TPU v7x, 32 devices: a whole 2x2x4 slice. The times are simulated.
32 devices in a mesh: gx: 4 (over y, x), gy: 4 (over z), gz: 2 (over core).
Axes of the slice: x: 2, y: 2, z: 4, core: 2. Of those that a mesh axis runs over, the one named last changes fastest.
Arguments:
- force: float32 [3, 128, 64, 256], P(None, 'gx', 'gy', 'gz'), may hold values from -6 to 6
- phase: int32 [128, 64, 256], P('gx', 'gy', 'gz'), may hold values from 0 to 7
- viscosity_table: float32 [8], replicated, may hold values from 0.1 to 10
- boundary_flags: int32 [6], replicated, may hold values from 0 to 1
Outputs:
- pressure: float32 [128, 64, 256], P('gx', 'gy', 'gz')
- residual: float32 [128, 64, 256], P('gx', 'gy', 'gz')
- res_norms: float32 [3], replicated
Inputs may be any that keep to these rules, and one draw needn't show every extreme that they name: phase ids index viscosity_table. `boundary_flags`: 0 marks a no-slip face, 1 a free-slip face.
All inputs are finite; a program needn't handle non-finite values.
Results may differ from a plain program's by a relative error of at most 0.0003.
Values sent between devices are 32-bit elements; how exact they have to be, the bound alone decides.
A program may use at most 192 MiB of HBM per device.

v0:
```python
import jax
import jax.numpy as jnp
from jax import lax
from jax.sharding import PartitionSpec as P

ITERS = 3
SWEEPS = 4
OMEGA = 0.8


def passed_along(value, axis, by):
    devices = lax.axis_size(axis)
    pairs = [(i, i + by) for i in range(devices) if 0 <= i + by < devices]
    return lax.ppermute(value, axis, pairs)


def extended(cells, sides, width):
    for axis, dim in sides:
        count = lax.axis_size(axis)
        ends = count - 1
        head = lax.slice_in_dim(cells, 0, width, axis=dim)
        tail = lax.slice_in_dim(cells, cells.shape[dim] - width, cells.shape[dim], axis=dim)
        cells = jnp.concatenate(
            [
                lax.ppermute(tail, axis, [(i, (i + 1) % count) for i in range(ends)]),
                cells,
                lax.ppermute(head, axis, [((i + 1) % count, i) for i in range(ends)]),
            ],
            axis=dim,
        )
    return cells


def lookup(phase, table):
    eta = jnp.zeros(phase.shape, jnp.float32)
    for level in range(table.shape[0]):
        eta = eta + jnp.where(phase == level, table[level], jnp.float32(0.0))
    return eta


def trim(array, keep):
    for dim in range(3):
        if dim != keep:
            array = lax.slice_in_dim(array, 1, array.shape[dim] - 1, axis=dim)
    return array


def coefficients(eta_wide, flags, starts, totals):
    walls = (flags == 0).astype(jnp.float32)
    inner = eta_wide[1:-1, 1:-1, 1:-1]
    faces = []
    diag = [jnp.zeros_like(inner) for comp in range(3)]
    for axis in range(3):
        length = eta_wide.shape[axis]
        spots = starts[axis] + jnp.arange(length, dtype=jnp.int32)
        inside = (spots >= 0) & (spots < totals[axis])
        shape = [1, 1, 1]
        shape[axis] = length - 2
        upper_in = inside[2:].reshape(shape)
        lower_in = inside[:-2].reshape(shape)
        sides = trim(eta_wide, axis)
        middle = lax.slice_in_dim(sides, 1, length - 1, axis=axis)
        upper = 0.5 * (middle + lax.slice_in_dim(sides, 2, length, axis=axis))
        lower = 0.5 * (middle + lax.slice_in_dim(sides, 0, length - 2, axis=axis))
        faces.append((jnp.where(upper_in, upper, 0.0), jnp.where(lower_in, lower, 0.0)))
        for comp in range(3):
            normal = 1.0 if comp == axis else 0.0
            wall_low = jnp.maximum(walls[2 * axis], normal)
            wall_high = jnp.maximum(walls[2 * axis + 1], normal)
            diag[comp] = (
                diag[comp]
                + jnp.where(upper_in, upper, wall_high * inner)
                + jnp.where(lower_in, lower, wall_low * inner)
            )
    return (faces, jnp.stack(diag))


def viscous(state, faces, diag):
    ends = []
    for axis, name in enumerate(("gx", "gy", "gz")):
        dim = axis + 1
        length = state.shape[dim]
        head = lax.slice_in_dim(state, 0, 1, axis=dim)
        tail = lax.slice_in_dim(state, length - 1, length, axis=dim)
        ends.append((passed_along(head, name, -1), passed_along(tail, name, 1)))
    result = diag * state
    for axis in range(3):
        dim = axis + 1
        length = state.shape[dim]
        above, below = ends[axis]
        upper = jnp.concatenate([lax.slice_in_dim(state, 1, length, axis=dim), above], dim)
        lower = jnp.concatenate([below, lax.slice_in_dim(state, 0, length - 1, axis=dim)], dim)
        result = result - faces[axis][0] * upper
        result = result - faces[axis][1] * lower
    return result


def gradient(field):
    upper_x = passed_along(field[0:1], "gx", -1)
    upper_y = passed_along(field[:, 0:1], "gy", -1)
    upper_z = passed_along(field[:, :, 0:1], "gz", -1)
    along_x = jnp.concatenate([field[1:], upper_x], 0) - field
    along_y = jnp.concatenate([field[:, 1:], upper_y], 1) - field
    along_z = jnp.concatenate([field[:, :, 1:], upper_z], 2) - field
    return jnp.stack([along_x, along_y, along_z])


def divergence(velocity):
    lower_x = passed_along(velocity[0][-1:], "gx", 1)
    lower_y = passed_along(velocity[1][:, -1:], "gy", 1)
    lower_z = passed_along(velocity[2][:, :, -1:], "gz", 1)
    total = jnp.concatenate([lower_x, velocity[0][:-1]], 0) - velocity[0]
    total = total + jnp.concatenate([lower_y, velocity[1][:, :-1]], 1) - velocity[1]
    total = total + jnp.concatenate([lower_z, velocity[2][:, :, :-1]], 2) - velocity[2]
    return total


def per_device(force, phase, viscosity_table, boundary_flags):
    rows = phase.shape
    totals = (
        rows[0] * lax.axis_size("gx"),
        rows[1] * lax.axis_size("gy"),
        rows[2] * lax.axis_size("gz"),
    )
    indices = (lax.axis_index("gx"), lax.axis_index("gy"), lax.axis_index("gz"))
    cells = float(totals[0] * totals[1] * totals[2])
    phase_wide = extended(phase, (("gx", 0), ("gy", 1), ("gz", 2)), 1)
    starts = tuple((indices[dim] * rows[dim] - 1 for dim in range(3)))
    eta_wide = lookup(phase_wide, viscosity_table)
    faces, diag = coefficients(eta_wide, boundary_flags, starts, totals)
    eta = eta_wide[1:-1, 1:-1, 1:-1]
    inverse = 1.0 / diag

    def sweeps(source, state, count):
        for sweep in range(count):
            state = state + OMEGA * inverse * (source - viscous(state, faces, diag))
        return state

    def schur(field):
        source = gradient(field)
        return divergence(sweeps(source, OMEGA * inverse * source, SWEEPS - 1))

    rhs = divergence(sweeps(force, OMEGA * inverse * force, SWEEPS - 1))
    pressure = jnp.zeros_like(rhs)
    residual = rhs
    norms = []
    scaled = eta * residual
    applied = schur(scaled)
    for step in range(ITERS):
        last = step + 1 == ITERS
        gamma, delta, squares = lax.psum(
            (jnp.sum(residual * scaled), jnp.sum(applied * scaled), jnp.sum(residual * residual)),
            ("gx", "gy", "gz"),
        )
        norms.append(squares / cells)
        if not last:
            mass_applied = eta * applied
            twice_applied = schur(mass_applied)
        if step == 0:
            alpha = gamma / delta
            search = scaled
            search_image = applied
            scaled_image = mass_applied
            applied_image = twice_applied
        else:
            beta = gamma / gamma_old
            alpha = gamma / (delta - beta * gamma / alpha_old)
            search = scaled + beta * search
            search_image = applied + beta * search_image
            if not last:
                scaled_image = mass_applied + beta * scaled_image
                applied_image = twice_applied + beta * applied_image
        pressure = pressure + alpha * search
        residual = residual - alpha * search_image
        if not last:
            scaled = scaled - alpha * scaled_image
            applied = applied - alpha * applied_image
        gamma_old = gamma
        alpha_old = alpha
    return (pressure, residual, jnp.stack(norms))


def solution(mesh):
    placed = (P(None, "gx", "gy", "gz"), P("gx", "gy", "gz"), P(), P())
    return jax.shard_map(
        per_device,
        mesh=mesh,
        in_specs=placed,
        out_specs=(P("gx", "gy", "gz"), P("gx", "gy", "gz"), P()),
        check_vma=False,
    )
```

profile of v0, /device:TPU:0, one launch (start us, length us, event | category | flops | bytes accessed | tf_op | source)
XLA Modules:
  0.0 667.3 jit_solution(11846374254720408442)
XLA Ops:
  2.6 5.5 collective-permute-start
  10.5 4.0 collective-permute-start.2
  16.5 3.7 collective-permute-done.3
  31.1 6.0 select_add_fusion
  47.0 3.0 collective-permute-start.11
  50.7 4.3 collective-permute-start.7
  56.2 3.5 collective-permute-start.9
  68.0 4.1 fusion.8
  78.7 3.6 collective-permute-start.17
  82.9 6.3 collective-permute-start.13
  90.5 4.5 collective-permute-start.15
  103.4 4.2 fusion.17
  114.4 3.6 collective-permute-start.23
  118.6 5.5 collective-permute-start.19
  125.3 4.5 collective-permute-start.21
  138.9 4.0 fusion.26
  143.0 4.9 collective-permute-start.24
  147.9 4.5 collective-permute-start.25
  152.6 3.1 collective-permute-start.26
  175.8 5.3 collective-permute-start.31
  182.4 4.5 collective-permute-start.33
  196.0 4.1 fusion.35
  206.7 4.2 collective-permute-start.41
  211.6 5.1 collective-permute-start.37
  218.0 4.5 collective-permute-start.39
  231.0 4.2 fusion.44
  241.9 3.6 collective-permute-start.47
  246.1 5.5 collective-permute-start.43
  252.8 4.5 collective-permute-start.45
  266.4 4.0 fusion.53
  270.5 4.9 collective-permute-start.48
  275.4 4.5 collective-permute-start.49
  280.1 3.2 collective-permute-start.50
  290.0 45.0 %all-reduce.2 = (f32[]{:T(128)}, f32[]{:T(128)}) all-reduce(f32[]{:T(128)} %get-tuple-element.14, f32[]{:T(128)} %get-tuple-element.13), channel_id=1, replica_groups=mesh['gx'=4,'gy'=4,'gz'=2] {'gx','gy','gz'}, use_global_device_ids=true, to_apply=%region_1.2 | all-reduce | flops 2 | bytes 16 | tf_op jit(solution)/shard_map/psum | solution.py:151
  346.7 4.8 collective-permute-start.55
  352.8 2.1 collective-permute-start.57
  363.9 4.1 fusion.62
  374.7 4.2 collective-permute-start.65
  379.5 5.1 collective-permute-start.61
  385.9 4.5 collective-permute-start.63
  399.1 4.2 fusion.71
  410.0 3.6 collective-permute-start.71
  414.2 5.1 collective-permute-start.67
  420.6 4.5 collective-permute-start.69
  434.2 4.0 fusion.80
  438.3 4.7 collective-permute-start.72
  443.0 4.5 collective-permute-start.73
  447.7 3.2 collective-permute-start.74
  457.7 44.4 %all-reduce.1 = (f32[]{:T(128)}, f32[]{:T(128)}) all-reduce(f32[]{:T(128)} %get-tuple-element.9, f32[]{:T(128)} %get-tuple-element.8), channel_id=1, replica_groups=mesh['gx'=4,'gy'=4,'gz'=2] {'gx','gy','gz'}, use_global_device_ids=true, to_apply=%region_5.6 | all-reduce | flops 2 | bytes 16 | tf_op jit(solution)/shard_map/psum | solution.py:151
  516.8 4.8 collective-permute-start.79
  522.9 3.8 collective-permute-start.81
  535.0 3.8 fusion.89
  543.6 3.0 collective-permute-start.89
  547.2 5.1 collective-permute-start.85
  553.6 4.5 collective-permute-start.87
  565.7 4.0 fusion.98
  576.3 3.6 collective-permute-start.95
  580.6 5.2 collective-permute-start.91
  587.0 4.5 collective-permute-start.93
  600.6 3.8 fusion.107
  604.5 4.7 collective-permute-start.96
  609.2 4.5 collective-permute-start.97
  613.9 3.2 collective-permute-start.98
  619.3 40.5 %all-reduce = (f32[]{:T(128)}, f32[]{:T(128)}, f32[]{:T(128)}, f32[]{:T(128)}, f32[]{:T(128)}) all-reduce(f32[]{:T(128)} %get-tuple-element.7, f32[]{:T(128)} %get-tuple-element.12, f32[]{:T(128)} %get-tuple-element.6, f32[]{:T(128)} %get-tuple-element.10, f32[]{:T(128)} %get-tuple-element.11), channel_id=1, replica_groups=mesh['gx'=4,'gy'=4,'gz'=2] {'gx','gy','gz'}, use_global_device_ids=true, to_apply=%region_9.10 | all-reduce | flops 5 | bytes 40 | tf_op jit(solution)/shard_map/psum | solution.py:151
  (484 shorter events, 253.3 us)
Async XLA Ops:
  1.3 9.1 %collective-permute-start.1 = (s32[1,16,128]{2,1,0:T(8,128)S(1)}, s32[1,16,128]{2,1,0:T(8,128)S(1)}, u32[]{:S(2)}, u32[]{:S(2)}) collective-permute-start(s32[1,16,128]{2,1,0:T(8,128)S(1)} %get-tuple-element.201), channel_id=1, source_target_pairs={{8,0},{16,8},{24,16},{9,1},{17,9},{25,17},{10,2},{18,10},{26,18},{... | collective-permute-start | bytes 24584 | tf_op jit(solution)/shard_map/ppermute | solution.py:27
  20.4 10.7 %collective-permute-start.4 = (s32[34,18,1]{2,1,0:T(8,128)S(1)}, s32[34,18,1]{2,1,0:T(8,128)S(1)}, u32[]{:S(2)}, u32[]{:S(2)}) collective-permute-start(s32[34,18,1]{2,1,0:T(8,128)S(1)} %get-tuple-element.188), channel_id=1, source_target_pairs={{0,1},{2,3},{4,5},{6,7},{8,9},{10,11},{12,13},{14,15},{16,17},{18,... | collective-permute-start | bytes 7352 | tf_op jit(solution)/shard_map/ppermute | solution.py:25
  21.8 9.4 %collective-permute-start.5 = (s32[34,18,1]{2,1,0:T(8,128)S(1)}, s32[34,18,1]{2,1,0:T(8,128)S(1)}, u32[]{:S(2)}, u32[]{:S(2)}) collective-permute-start(s32[34,18,1]{2,1,0:T(8,128)S(1)} %get-tuple-element.189), channel_id=1, source_target_pairs={{1,0},{3,2},{5,4},{7,6},{9,8},{11,10},{13,12},{15,14},{17,16},{19,... | collective-permute-start | bytes 7352 | tf_op jit(solution)/shard_map/ppermute | solution.py:27
  47.0 14.5 %collective-permute-start.11 = (f32[3,32,16,1]{1,2,3,0:T(8,128)S(1)}, f32[3,32,16,1]{1,2,3,0:T(8,128)S(1)}, u32[]{:S(2)}, u32[]{:S(2)}) collective-permute-start(f32[3,32,16,1]{1,2,3,0:T(8,128)S(1)} %copy.22), channel_id=1, source_target_pairs={{0,1},{2,3},{4,5},{6,7},{8,9},{10,11},{12,13},{14,15},{16,17},{18,... | collective-permute-start | bytes 18440 | tf_op jit(solution)/shard_map/ppermute | solution.py:14
  50.7 16.7 %collective-permute-start.7 = (f32[3,1,16,128]{3,2,1,0:T(8,128)}, f32[3,1,16,128]{3,2,1,0:T(8,128)S(1)}, u32[]{:S(2)}, u32[]{:S(2)}) collective-permute-start(f32[3,1,16,128]{3,2,1,0:T(8,128)} %get-tuple-element.184), channel_id=1, source_target_pairs={{0,8},{8,16},{16,24},{1,9},{9,17},{17,25},{2,10},{10,18},{18,26},{... | collective-permute-start | bytes 73736 | tf_op jit(solution)/shard_map/ppermute | solution.py:14
  54.9 12.4 %collective-permute-start.6 = (f32[3,1,16,128]{3,2,1,0:T(8,128)}, f32[3,1,16,128]{3,2,1,0:T(8,128)S(1)}, u32[]{:S(2)}, u32[]{:S(2)}) collective-permute-start(f32[3,1,16,128]{3,2,1,0:T(8,128)} %get-tuple-element.185), channel_id=1, source_target_pairs={{8,0},{16,8},{24,16},{9,1},{17,9},{25,17},{10,2},{18,10},{26,18},{... | collective-permute-start | bytes 73736 | tf_op jit(solution)/shard_map/ppermute | solution.py:14
  56.2 11.1 %collective-permute-start.9 = (f32[3,32,1,128]{3,2,1,0:T(1,128)}, f32[3,32,1,128]{3,2,1,0:T(1,128)S(1)}, u32[]{:S(2)}, u32[]{:S(2)}) collective-permute-start(f32[3,32,1,128]{3,2,1,0:T(1,128)} %get-tuple-element.180), channel_id=1, source_target_pairs={{0,2},{2,4},{4,6},{1,3},{3,5},{5,7},{8,10},{10,12},{12,14},{9,11},... | collective-permute-start | bytes 147464 | tf_op jit(solution)/shard_map/ppermute | solution.py:14
  78.7 18.7 %collective-permute-start.17 = (f32[3,32,16,1]{1,2,3,0:T(8,128)}, f32[3,32,16,1]{1,2,3,0:T(8,128)}, u32[]{:S(2)}, u32[]{:S(2)}) collective-permute-start(f32[3,32,16,1]{1,2,3,0:T(8,128)} %copy.26), channel_id=1, source_target_pairs={{0,1},{2,3},{4,5},{6,7},{8,9},{10,11},{12,13},{14,15},{16,17},{18,... | collective-permute-start | bytes 18440 | tf_op jit(solution)/shard_map/ppermute | solution.py:14
  82.9 20.5 %collective-permute-start.13 = (f32[3,1,16,128]{3,2,1,0:T(8,128)}, f32[3,1,16,128]{3,2,1,0:T(8,128)}, u32[]{:S(2)}, u32[]{:S(2)}) collective-permute-start(f32[3,1,16,128]{3,2,1,0:T(8,128)} %get-tuple-element.172), channel_id=1, source_target_pairs={{0,8},{8,16},{16,24},{1,9},{9,17},{17,25},{2,10},{10,18},{18,26},{... | collective-permute-start | bytes 73736 | tf_op jit(solution)/shard_map/ppermute | solution.py:14
  89.2 14.2 %collective-permute-start.12 = (f32[3,1,16,128]{3,2,1,0:T(8,128)}, f32[3,1,16,128]{3,2,1,0:T(8,128)}, u32[]{:S(2)}, u32[]{:S(2)}) collective-permute-start(f32[3,1,16,128]{3,2,1,0:T(8,128)} %get-tuple-element.173), channel_id=1, source_target_pairs={{8,0},{16,8},{24,16},{9,1},{17,9},{25,17},{10,2},{18,10},{26,18},{... | collective-permute-start | bytes 73736 | tf_op jit(solution)/shard_map/ppermute | solution.py:14
  90.5 12.9 %collective-permute-start.15 = (f32[3,32,1,128]{3,2,1,0:T(1,128)}, f32[3,32,1,128]{3,2,1,0:T(1,128)S(1)}, u32[]{:S(2)}, u32[]{:S(2)}) collective-permute-start(f32[3,32,1,128]{3,2,1,0:T(1,128)} %get-tuple-element.168), channel_id=1, source_target_pairs={{0,2},{2,4},{4,6},{1,3},{3,5},{5,7},{8,10},{10,12},{12,14},{9,11},... | collective-permute-start | bytes 147464 | tf_op jit(solution)/shard_map/ppermute | solution.py:14
  114.4 17.8 %collective-permute-start.23 = (f32[3,32,16,1]{1,2,3,0:T(8,128)}, f32[3,32,16,1]{1,2,3,0:T(8,128)}, u32[]{:S(2)}, u32[]{:S(2)}) collective-permute-start(f32[3,32,16,1]{1,2,3,0:T(8,128)} %copy.30), channel_id=1, source_target_pairs={{0,1},{2,3},{4,5},{6,7},{8,9},{10,11},{12,13},{14,15},{16,17},{18,... | collective-permute-start | bytes 18440 | tf_op jit(solution)/shard_map/ppermute | solution.py:14
  118.6 20.3 %collective-permute-start.19 = (f32[3,1,16,128]{3,2,1,0:T(8,128)}, f32[3,1,16,128]{3,2,1,0:T(8,128)}, u32[]{:S(2)}, u32[]{:S(2)}) collective-permute-start(f32[3,1,16,128]{3,2,1,0:T(8,128)} %get-tuple-element.160), channel_id=1, source_target_pairs={{0,8},{8,16},{16,24},{1,9},{9,17},{17,25},{2,10},{10,18},{18,26},{... | collective-permute-start | bytes 73736 | tf_op jit(solution)/shard_map/ppermute | solution.py:14
  124.0 14.8 %collective-permute-start.18 = (f32[3,1,16,128]{3,2,1,0:T(8,128)}, f32[3,1,16,128]{3,2,1,0:T(8,128)}, u32[]{:S(2)}, u32[]{:S(2)}) collective-permute-start(f32[3,1,16,128]{3,2,1,0:T(8,128)} %get-tuple-element.161), channel_id=1, source_target_pairs={{8,0},{16,8},{24,16},{9,1},{17,9},{25,17},{10,2},{18,10},{26,18},{... | collective-permute-start | bytes 73736 | tf_op jit(solution)/shard_map/ppermute | solution.py:14
  125.3 13.5 %collective-permute-start.21 = (f32[3,32,1,128]{3,2,1,0:T(1,128)}, f32[3,32,1,128]{3,2,1,0:T(1,128)S(1)}, u32[]{:S(2)}, u32[]{:S(2)}) collective-permute-start(f32[3,32,1,128]{3,2,1,0:T(1,128)} %get-tuple-element.156), channel_id=1, source_target_pairs={{0,2},{2,4},{4,6},{1,3},{3,5},{5,7},{8,10},{10,12},{12,14},{9,11},... | collective-permute-start | bytes 147464 | tf_op jit(solution)/shard_map/ppermute | solution.py:14
  143.0 13.8 %collective-permute-start.24 = (f32[1,16,128]{2,1,0:T(8,128)S(1)}, f32[1,16,128]{2,1,0:T(8,128)S(1)}, u32[]{:S(2)}, u32[]{:S(2)}) collective-permute-start(f32[1,16,128]{2,1,0:T(8,128)S(1)} %slice_bitcast_fusion.19), channel_id=1, source_target_pairs={{0,8},{8,16},{16,24},{1,9},{9,17},{17,25},{2,10},{10,18},{18,26},{... | collective-permute-start | bytes 24584 | tf_op jit(solution)/shard_map/ppermute | solution.py:14
  173.2 16.0 %collective-permute-start.35 = (f32[3,32,16,1]{1,2,3,0:T(8,128)}, f32[3,32,16,1]{1,2,3,0:T(8,128)}, u32[]{:S(2)}, u32[]{:S(2)}) collective-permute-start(f32[3,32,16,1]{1,2,3,0:T(8,128)} %copy.34), channel_id=1, source_target_pairs={{0,1},{2,3},{4,5},{6,7},{8,9},{10,11},{12,13},{14,15},{16,17},{18,... | collective-permute-start | bytes 18440 | tf_op jit(solution)/shard_map/ppermute | solution.py:14
  175.8 20.1 %collective-permute-start.31 = (f32[3,1,16,128]{3,2,1,0:T(8,128)}, f32[3,1,16,128]{3,2,1,0:T(8,128)}, u32[]{:S(2)}, u32[]{:S(2)}) collective-permute-start(f32[3,1,16,128]{3,2,1,0:T(8,128)} %get-tuple-element.146), channel_id=1, source_target_pairs={{0,8},{8,16},{16,24},{1,9},{9,17},{17,25},{2,10},{10,18},{18,26},{... | collective-permute-start | bytes 73736 | tf_op jit(solution)/shard_map/ppermute | solution.py:14
  181.1 14.8 %collective-permute-start.30 = (f32[3,1,16,128]{3,2,1,0:T(8,128)}, f32[3,1,16,128]{3,2,1,0:T(8,128)}, u32[]{:S(2)}, u32[]{:S(2)}) collective-permute-start(f32[3,1,16,128]{3,2,1,0:T(8,128)} %get-tuple-element.147), channel_id=1, source_target_pairs={{8,0},{16,8},{24,16},{9,1},{17,9},{25,17},{10,2},{18,10},{26,18},{... | collective-permute-start | bytes 73736 | tf_op jit(solution)/shard_map/ppermute | solution.py:14
  182.4 13.5 %collective-permute-start.33 = (f32[3,32,1,128]{3,2,1,0:T(1,128)}, f32[3,32,1,128]{3,2,1,0:T(1,128)S(1)}, u32[]{:S(2)}, u32[]{:S(2)}) collective-permute-start(f32[3,32,1,128]{3,2,1,0:T(1,128)} %get-tuple-element.142), channel_id=1, source_target_pairs={{0,2},{2,4},{4,6},{1,3},{3,5},{5,7},{8,10},{10,12},{12,14},{9,11},... | collective-permute-start | bytes 147464 | tf_op jit(solution)/shard_map/ppermute | solution.py:14
  206.7 18.1 %collective-permute-start.41 = (f32[3,32,16,1]{1,2,3,0:T(8,128)}, f32[3,32,16,1]{1,2,3,0:T(8,128)}, u32[]{:S(2)}, u32[]{:S(2)}) collective-permute-start(f32[3,32,16,1]{1,2,3,0:T(8,128)} %copy.38), channel_id=1, source_target_pairs={{0,1},{2,3},{4,5},{6,7},{8,9},{10,11},{12,13},{14,15},{16,17},{18,... | collective-permute-start | bytes 18440 | tf_op jit(solution)/shard_map/ppermute | solution.py:14
  211.6 19.4 %collective-permute-start.37 = (f32[3,1,16,128]{3,2,1,0:T(8,128)}, f32[3,1,16,128]{3,2,1,0:T(8,128)}, u32[]{:S(2)}, u32[]{:S(2)}) collective-permute-start(f32[3,1,16,128]{3,2,1,0:T(8,128)} %get-tuple-element.134), channel_id=1, source_target_pairs={{0,8},{8,16},{16,24},{1,9},{9,17},{17,25},{2,10},{10,18},{18,26},{... | collective-permute-start | bytes 73736 | tf_op jit(solution)/shard_map/ppermute | solution.py:14
  216.7 14.2 %collective-permute-start.36 = (f32[3,1,16,128]{3,2,1,0:T(8,128)}, f32[3,1,16,128]{3,2,1,0:T(8,128)}, u32[]{:S(2)}, u32[]{:S(2)}) collective-permute-start(f32[3,1,16,128]{3,2,1,0:T(8,128)} %get-tuple-element.135), channel_id=1, source_target_pairs={{8,0},{16,8},{24,16},{9,1},{17,9},{25,17},{10,2},{18,10},{26,18},{... | collective-permute-start | bytes 73736 | tf_op jit(solution)/shard_map/ppermute | solution.py:14
  218.0 12.9 %collective-permute-start.39 = (f32[3,32,1,128]{3,2,1,0:T(1,128)}, f32[3,32,1,128]{3,2,1,0:T(1,128)S(1)}, u32[]{:S(2)}, u32[]{:S(2)}) collective-permute-start(f32[3,32,1,128]{3,2,1,0:T(1,128)} %get-tuple-element.130), channel_id=1, source_target_pairs={{0,2},{2,4},{4,6},{1,3},{3,5},{5,7},{8,10},{10,12},{12,14},{9,11},... | collective-permute-start | bytes 147464 | tf_op jit(solution)/shard_map/ppermute | solution.py:14
  241.9 17.8 %collective-permute-start.47 = (f32[3,32,16,1]{1,2,3,0:T(8,128)}, f32[3,32,16,1]{1,2,3,0:T(8,128)}, u32[]{:S(2)}, u32[]{:S(2)}) collective-permute-start(f32[3,32,16,1]{1,2,3,0:T(8,128)} %copy.42), channel_id=1, source_target_pairs={{0,1},{2,3},{4,5},{6,7},{8,9},{10,11},{12,13},{14,15},{16,17},{18,... | collective-permute-start | bytes 18440 | tf_op jit(solution)/shard_map/ppermute | solution.py:14
  246.1 20.3 %collective-permute-start.43 = (f32[3,1,16,128]{3,2,1,0:T(8,128)}, f32[3,1,16,128]{3,2,1,0:T(8,128)}, u32[]{:S(2)}, u32[]{:S(2)}) collective-permute-start(f32[3,1,16,128]{3,2,1,0:T(8,128)} %get-tuple-element.122), channel_id=1, source_target_pairs={{0,8},{8,16},{16,24},{1,9},{9,17},{17,25},{2,10},{10,18},{18,26},{... | collective-permute-start | bytes 73736 | tf_op jit(solution)/shard_map/ppermute | solution.py:14
  251.6 14.8 %collective-permute-start.42 = (f32[3,1,16,128]{3,2,1,0:T(8,128)}, f32[3,1,16,128]{3,2,1,0:T(8,128)}, u32[]{:S(2)}, u32[]{:S(2)}) collective-permute-start(f32[3,1,16,128]{3,2,1,0:T(8,128)} %get-tuple-element.123), channel_id=1, source_target_pairs={{8,0},{16,8},{24,16},{9,1},{17,9},{25,17},{10,2},{18,10},{26,18},{... | collective-permute-start | bytes 73736 | tf_op jit(solution)/shard_map/ppermute | solution.py:14
  252.8 13.5 %collective-permute-start.45 = (f32[3,32,1,128]{3,2,1,0:T(1,128)}, f32[3,32,1,128]{3,2,1,0:T(1,128)S(1)}, u32[]{:S(2)}, u32[]{:S(2)}) collective-permute-start(f32[3,32,1,128]{3,2,1,0:T(1,128)} %get-tuple-element.118), channel_id=1, source_target_pairs={{0,2},{2,4},{4,6},{1,3},{3,5},{5,7},{8,10},{10,12},{12,14},{9,11},... | collective-permute-start | bytes 147464 | tf_op jit(solution)/shard_map/ppermute | solution.py:14
  270.5 14.0 %collective-permute-start.48 = (f32[1,16,128]{2,1,0:T(8,128)S(1)}, f32[1,16,128]{2,1,0:T(8,128)S(1)}, u32[]{:S(2)}, u32[]{:S(2)}) collective-permute-start(f32[1,16,128]{2,1,0:T(8,128)S(1)} %slice_bitcast_fusion.18), channel_id=1, source_target_pairs={{0,8},{8,16},{16,24},{1,9},{9,17},{17,25},{2,10},{10,18},{18,26},{... | collective-permute-start | bytes 24584 | tf_op jit(solution)/shard_map/ppermute | solution.py:14
  275.4 9.1 %collective-permute-start.49 = (f32[32,1,128]{2,1,0:T(1,128)S(1)}, f32[32,1,128]{2,1,0:T(1,128)S(1)}, u32[]{:S(2)}, u32[]{:S(2)}) collective-permute-start(f32[32,1,128]{2,1,0:T(1,128)S(1)} %slice.1124), channel_id=1, source_target_pairs={{0,2},{2,4},{4,6},{1,3},{3,5},{5,7},{8,10},{10,12},{12,14},{9,11},... | collective-permute-start | bytes 49160 | tf_op jit(solution)/shard_map/ppermute | solution.py:14
  286.0 50.4 %collective-permute-start.52 = (f32[32,1,128]{2,1,0:T(1,128)S(1)}, f32[32,1,128]{2,1,0:T(1,128)S(1)}, u32[]{:S(2)}, u32[]{:S(2)}) collective-permute-start(f32[32,1,128]{2,1,0:T(1,128)S(1)} %slice.1132), channel_id=1, source_target_pairs={{2,0},{4,2},{6,4},{3,1},{5,3},{7,5},{10,8},{12,10},{14,12},{11,9},... | collective-permute-start | bytes 49160 | tf_op jit(solution)/shard_map/ppermute | solution.py:14
  287.4 49.1 %collective-permute-start.51 = (f32[1,16,128]{2,1,0:T(8,128)S(1)}, f32[1,16,128]{2,1,0:T(8,128)S(1)}, u32[]{:S(2)}, u32[]{:S(2)}) collective-permute-start(f32[1,16,128]{2,1,0:T(8,128)S(1)} %slice.1130), channel_id=1, source_target_pairs={{8,0},{16,8},{24,16},{9,1},{17,9},{25,17},{10,2},{18,10},{26,18},{... | collective-permute-start | bytes 24584 | tf_op jit(solution)/shard_map/ppermute | solution.py:14
  288.7 47.8 %collective-permute-start.53 = (f32[32,16,1]{2,1,0:T(8,128)S(1)}, f32[32,16,1]{2,1,0:T(8,128)S(1)}, u32[]{:S(2)}, u32[]{:S(2)}) collective-permute-start(f32[32,16,1]{2,1,0:T(8,128)S(1)} %bitcast.173), channel_id=1, source_target_pairs={{1,0},{3,2},{5,4},{7,6},{9,8},{11,10},{13,12},{15,14},{17,16},{19,... | collective-permute-start | bytes 6152 | tf_op jit(solution)/shard_map/ppermute | solution.py:14
  344.2 13.0 %collective-permute-start.59 = (f32[3,32,16,1]{1,2,3,0:T(8,128)}, f32[3,32,16,1]{1,2,3,0:T(8,128)}, u32[]{:S(2)}, u32[]{:S(2)}) collective-permute-start(f32[3,32,16,1]{1,2,3,0:T(8,128)} %copy.46), channel_id=1, source_target_pairs={{0,1},{2,3},{4,5},{6,7},{8,9},{10,11},{12,13},{14,15},{16,17},{18,... | collective-permute-start | bytes 18440 | tf_op jit(solution)/shard_map/ppermute | solution.py:14
  346.7 17.2 %collective-permute-start.55 = (f32[3,1,16,128]{3,2,1,0:T(8,128)}, f32[3,1,16,128]{3,2,1,0:T(8,128)}, u32[]{:S(2)}, u32[]{:S(2)}) collective-permute-start(f32[3,1,16,128]{3,2,1,0:T(8,128)} %get-tuple-element.108), channel_id=1, source_target_pairs={{0,8},{8,16},{16,24},{1,9},{9,17},{17,25},{2,10},{10,18},{18,26},{... | collective-permute-start | bytes 73736 | tf_op jit(solution)/shard_map/ppermute | solution.py:14
  351.5 12.4 %collective-permute-start.54 = (f32[3,1,16,128]{3,2,1,0:T(8,128)}, f32[3,1,16,128]{3,2,1,0:T(8,128)}, u32[]{:S(2)}, u32[]{:S(2)}) collective-permute-start(f32[3,1,16,128]{3,2,1,0:T(8,128)} %get-tuple-element.109), channel_id=1, source_target_pairs={{8,0},{16,8},{24,16},{9,1},{17,9},{25,17},{10,2},{18,10},{26,18},{... | collective-permute-start | bytes 73736 | tf_op jit(solution)/shard_map/ppermute | solution.py:14
  352.8 11.1 %collective-permute-start.57 = (f32[3,32,1,128]{3,2,1,0:T(1,128)}, f32[3,32,1,128]{3,2,1,0:T(1,128)S(1)}, u32[]{:S(2)}, u32[]{:S(2)}) collective-permute-start(f32[3,32,1,128]{3,2,1,0:T(1,128)} %get-tuple-element.104), channel_id=1, source_target_pairs={{0,2},{2,4},{4,6},{1,3},{3,5},{5,7},{8,10},{10,12},{12,14},{9,11},... | collective-permute-start | bytes 147464 | tf_op jit(solution)/shard_map/ppermute | solution.py:14
  374.7 18.5 %collective-permute-start.65 = (f32[3,32,16,1]{1,2,3,0:T(8,128)}, f32[3,32,16,1]{1,2,3,0:T(8,128)}, u32[]{:S(2)}, u32[]{:S(2)}) collective-permute-start(f32[3,32,16,1]{1,2,3,0:T(8,128)} %copy.50), channel_id=1, source_target_pairs={{0,1},{2,3},{4,5},{6,7},{8,9},{10,11},{12,13},{14,15},{16,17},{18,... | collective-permute-start | bytes 18440 | tf_op jit(solution)/shard_map/ppermute | solution.py:14
  379.5 19.6 %collective-permute-start.61 = (f32[3,1,16,128]{3,2,1,0:T(8,128)}, f32[3,1,16,128]{3,2,1,0:T(8,128)}, u32[]{:S(2)}, u32[]{:S(2)}) collective-permute-start(f32[3,1,16,128]{3,2,1,0:T(8,128)} %get-tuple-element.96), channel_id=1, source_target_pairs={{0,8},{8,16},{16,24},{1,9},{9,17},{17,25},{2,10},{10,18},{18,26},{... | collective-permute-start | bytes 73736 | tf_op jit(solution)/shard_map/ppermute | solution.py:14
  384.6 14.4 %collective-permute-start.60 = (f32[3,1,16,128]{3,2,1,0:T(8,128)}, f32[3,1,16,128]{3,2,1,0:T(8,128)}, u32[]{:S(2)}, u32[]{:S(2)}) collective-permute-start(f32[3,1,16,128]{3,2,1,0:T(8,128)} %get-tuple-element.97), channel_id=1, source_target_pairs={{8,0},{16,8},{24,16},{9,1},{17,9},{25,17},{10,2},{18,10},{26,18},{... | collective-permute-start | bytes 73736 | tf_op jit(solution)/shard_map/ppermute | solution.py:14
  385.9 13.1 %collective-permute-start.63 = (f32[3,32,1,128]{3,2,1,0:T(1,128)}, f32[3,32,1,128]{3,2,1,0:T(1,128)S(1)}, u32[]{:S(2)}, u32[]{:S(2)}) collective-permute-start(f32[3,32,1,128]{3,2,1,0:T(1,128)} %get-tuple-element.92), channel_id=1, source_target_pairs={{0,2},{2,4},{4,6},{1,3},{3,5},{5,7},{8,10},{10,12},{12,14},{9,11},... | collective-permute-start | bytes 147464 | tf_op jit(solution)/shard_map/ppermute | solution.py:14
  410.0 17.5 %collective-permute-start.71 = (f32[3,32,16,1]{1,2,3,0:T(8,128)}, f32[3,32,16,1]{1,2,3,0:T(8,128)}, u32[]{:S(2)}, u32[]{:S(2)}) collective-permute-start(f32[3,32,16,1]{1,2,3,0:T(8,128)} %copy.54), channel_id=1, source_target_pairs={{0,1},{2,3},{4,5},{6,7},{8,9},{10,11},{12,13},{14,15},{16,17},{18,... | collective-permute-start | bytes 18440 | tf_op jit(solution)/shard_map/ppermute | solution.py:14
  414.2 20.0 %collective-permute-start.67 = (f32[3,1,16,128]{3,2,1,0:T(8,128)}, f32[3,1,16,128]{3,2,1,0:T(8,128)}, u32[]{:S(2)}, u32[]{:S(2)}) collective-permute-start(f32[3,1,16,128]{3,2,1,0:T(8,128)} %get-tuple-element.84), channel_id=1, source_target_pairs={{0,8},{8,16},{16,24},{1,9},{9,17},{17,25},{2,10},{10,18},{18,26},{... | collective-permute-start | bytes 73736 | tf_op jit(solution)/shard_map/ppermute | solution.py:14
  419.3 14.8 %collective-permute-start.66 = (f32[3,1,16,128]{3,2,1,0:T(8,128)}, f32[3,1,16,128]{3,2,1,0:T(8,128)}, u32[]{:S(2)}, u32[]{:S(2)}) collective-permute-start(f32[3,1,16,128]{3,2,1,0:T(8,128)} %get-tuple-element.85), channel_id=1, source_target_pairs={{8,0},{16,8},{24,16},{9,1},{17,9},{25,17},{10,2},{18,10},{26,18},{... | collective-permute-start | bytes 73736 | tf_op jit(solution)/shard_map/ppermute | solution.py:14
  420.6 13.5 %collective-permute-start.69 = (f32[3,32,1,128]{3,2,1,0:T(1,128)}, f32[3,32,1,128]{3,2,1,0:T(1,128)S(1)}, u32[]{:S(2)}, u32[]{:S(2)}) collective-permute-start(f32[3,32,1,128]{3,2,1,0:T(1,128)} %get-tuple-element.80), channel_id=1, source_target_pairs={{0,2},{2,4},{4,6},{1,3},{3,5},{5,7},{8,10},{10,12},{12,14},{9,11},... | collective-permute-start | bytes 147464 | tf_op jit(solution)/shard_map/ppermute | solution.py:14
  438.3 13.8 %collective-permute-start.72 = (f32[1,16,128]{2,1,0:T(8,128)S(1)}, f32[1,16,128]{2,1,0:T(8,128)S(1)}, u32[]{:S(2)}, u32[]{:S(2)}) collective-permute-start(f32[1,16,128]{2,1,0:T(8,128)S(1)} %slice_bitcast_fusion.17), channel_id=1, source_target_pairs={{0,8},{8,16},{16,24},{1,9},{9,17},{17,25},{2,10},{10,18},{18,26},{... | collective-permute-start | bytes 24584 | tf_op jit(solution)/shard_map/ppermute | solution.py:14
  443.0 9.1 %collective-permute-start.73 = (f32[32,1,128]{2,1,0:T(1,128)S(1)}, f32[32,1,128]{2,1,0:T(1,128)S(1)}, u32[]{:S(2)}, u32[]{:S(2)}) collective-permute-start(f32[32,1,128]{2,1,0:T(1,128)S(1)} %slice.1175), channel_id=1, source_target_pairs={{0,2},{2,4},{4,6},{1,3},{3,5},{5,7},{8,10},{10,12},{12,14},{9,11},... | collective-permute-start | bytes 49160 | tf_op jit(solution)/shard_map/ppermute | solution.py:14
  453.8 52.8 %collective-permute-start.76 = (f32[32,1,128]{2,1,0:T(1,128)S(1)}, f32[32,1,128]{2,1,0:T(1,128)S(1)}, u32[]{:S(2)}, u32[]{:S(2)}) collective-permute-start(f32[32,1,128]{2,1,0:T(1,128)S(1)} %slice.1183), channel_id=1, source_target_pairs={{2,0},{4,2},{6,4},{3,1},{5,3},{7,5},{10,8},{12,10},{14,12},{11,9},... | collective-permute-start | bytes 49160 | tf_op jit(solution)/shard_map/ppermute | solution.py:14
  455.1 51.5 %collective-permute-start.75 = (f32[1,16,128]{2,1,0:T(8,128)S(1)}, f32[1,16,128]{2,1,0:T(8,128)S(1)}, u32[]{:S(2)}, u32[]{:S(2)}) collective-permute-start(f32[1,16,128]{2,1,0:T(8,128)S(1)} %slice.1181), channel_id=1, source_target_pairs={{8,0},{16,8},{24,16},{9,1},{17,9},{25,17},{10,2},{18,10},{26,18},{... | collective-permute-start | bytes 24584 | tf_op jit(solution)/shard_map/ppermute | solution.py:14
  456.4 50.2 %collective-permute-start.77 = (f32[32,16,1]{2,1,0:T(8,128)S(1)}, f32[32,16,1]{2,1,0:T(8,128)S(1)}, u32[]{:S(2)}, u32[]{:S(2)}) collective-permute-start(f32[32,16,1]{2,1,0:T(8,128)S(1)} %bitcast.174), channel_id=1, source_target_pairs={{1,0},{3,2},{5,4},{7,6},{9,8},{11,10},{13,12},{15,14},{17,16},{19,... | collective-permute-start | bytes 6152 | tf_op jit(solution)/shard_map/ppermute | solution.py:14
  514.3 14.6 %collective-permute-start.83 = (f32[3,32,16,1]{1,2,3,0:T(8,128)}, f32[3,32,16,1]{1,2,3,0:T(8,128)}, u32[]{:S(2)}, u32[]{:S(2)}) collective-permute-start(f32[3,32,16,1]{1,2,3,0:T(8,128)} %copy.58), channel_id=1, source_target_pairs={{0,1},{2,3},{4,5},{6,7},{8,9},{10,11},{12,13},{14,15},{16,17},{18,... | collective-permute-start | bytes 18440 | tf_op jit(solution)/shard_map/ppermute | solution.py:14
  516.8 18.2 %collective-permute-start.79 = (f32[3,1,16,128]{3,2,1,0:T(8,128)}, f32[3,1,16,128]{3,2,1,0:T(8,128)}, u32[]{:S(2)}, u32[]{:S(2)}) collective-permute-start(f32[3,1,16,128]{3,2,1,0:T(8,128)} %get-tuple-element.70), channel_id=1, source_target_pairs={{0,8},{8,16},{16,24},{1,9},{9,17},{17,25},{2,10},{10,18},{18,26},{... | collective-permute-start | bytes 73736 | tf_op jit(solution)/shard_map/ppermute | solution.py:14
  521.6 13.4 %collective-permute-start.78 = (f32[3,1,16,128]{3,2,1,0:T(8,128)}, f32[3,1,16,128]{3,2,1,0:T(8,128)}, u32[]{:S(2)}, u32[]{:S(2)}) collective-permute-start(f32[3,1,16,128]{3,2,1,0:T(8,128)} %get-tuple-element.71), channel_id=1, source_target_pairs={{8,0},{16,8},{24,16},{9,1},{17,9},{25,17},{10,2},{18,10},{26,18},{... | collective-permute-start | bytes 73736 | tf_op jit(solution)/shard_map/ppermute | solution.py:14
  522.9 12.1 %collective-permute-start.81 = (f32[3,32,1,128]{3,2,1,0:T(1,128)}, f32[3,32,1,128]{3,2,1,0:T(1,128)S(1)}, u32[]{:S(2)}, u32[]{:S(2)}) collective-permute-start(f32[3,32,1,128]{3,2,1,0:T(1,128)} %get-tuple-element.66), channel_id=1, source_target_pairs={{0,2},{2,4},{4,6},{1,3},{3,5},{5,7},{8,10},{10,12},{12,14},{9,11},... | collective-permute-start | bytes 147464 | tf_op jit(solution)/shard_map/ppermute | solution.py:14
  543.6 16.9 %collective-permute-start.89 = (f32[3,32,16,1]{1,2,3,0:T(8,128)}, f32[3,32,16,1]{1,2,3,0:T(8,128)S(1)}, u32[]{:S(2)}, u32[]{:S(2)}) collective-permute-start(f32[3,32,16,1]{1,2,3,0:T(8,128)} %copy.62), channel_id=1, source_target_pairs={{0,1},{2,3},{4,5},{6,7},{8,9},{10,11},{12,13},{14,15},{16,17},{18,... | collective-permute-start | bytes 18440 | tf_op jit(solution)/shard_map/ppermute | solution.py:14
  547.2 18.4 %collective-permute-start.85 = (f32[3,1,16,128]{3,2,1,0:T(8,128)}, f32[3,1,16,128]{3,2,1,0:T(8,128)}, u32[]{:S(2)}, u32[]{:S(2)}) collective-permute-start(f32[3,1,16,128]{3,2,1,0:T(8,128)} %get-tuple-element.58), channel_id=1, source_target_pairs={{0,8},{8,16},{16,24},{1,9},{9,17},{17,25},{2,10},{10,18},{18,26},{... | collective-permute-start | bytes 73736 | tf_op jit(solution)/shard_map/ppermute | solution.py:14
  552.4 13.3 %collective-permute-start.84 = (f32[3,1,16,128]{3,2,1,0:T(8,128)}, f32[3,1,16,128]{3,2,1,0:T(8,128)}, u32[]{:S(2)}, u32[]{:S(2)}) collective-permute-start(f32[3,1,16,128]{3,2,1,0:T(8,128)} %get-tuple-element.59), channel_id=1, source_target_pairs={{8,0},{16,8},{24,16},{9,1},{17,9},{25,17},{10,2},{18,10},{26,18},{... | collective-permute-start | bytes 73736 | tf_op jit(solution)/shard_map/ppermute | solution.py:14
  553.6 12.0 %collective-permute-start.87 = (f32[3,32,1,128]{3,2,1,0:T(1,128)}, f32[3,32,1,128]{3,2,1,0:T(1,128)S(1)}, u32[]{:S(2)}, u32[]{:S(2)}) collective-permute-start(f32[3,32,1,128]{3,2,1,0:T(1,128)} %get-tuple-element.54), channel_id=1, source_target_pairs={{0,2},{2,4},{4,6},{1,3},{3,5},{5,7},{8,10},{10,12},{12,14},{9,11},... | collective-permute-start | bytes 147464 | tf_op jit(solution)/shard_map/ppermute | solution.py:14
  576.3 17.5 %collective-permute-start.95 = (f32[3,32,16,1]{1,2,3,0:T(8,128)}, f32[3,32,16,1]{1,2,3,0:T(8,128)}, u32[]{:S(2)}, u32[]{:S(2)}) collective-permute-start(f32[3,32,16,1]{1,2,3,0:T(8,128)} %copy.66), channel_id=1, source_target_pairs={{0,1},{2,3},{4,5},{6,7},{8,9},{10,11},{12,13},{14,15},{16,17},{18,... | collective-permute-start | bytes 18440 | tf_op jit(solution)/shard_map/ppermute | solution.py:14
  580.6 20.0 %collective-permute-start.91 = (f32[3,1,16,128]{3,2,1,0:T(8,128)}, f32[3,1,16,128]{3,2,1,0:T(8,128)}, u32[]{:S(2)}, u32[]{:S(2)}) collective-permute-start(f32[3,1,16,128]{3,2,1,0:T(8,128)} %get-tuple-element.46), channel_id=1, source_target_pairs={{0,8},{8,16},{16,24},{1,9},{9,17},{17,25},{2,10},{10,18},{18,26},{... | collective-permute-start | bytes 73736 | tf_op jit(solution)/shard_map/ppermute | solution.py:14
  585.7 14.8 %collective-permute-start.90 = (f32[3,1,16,128]{3,2,1,0:T(8,128)}, f32[3,1,16,128]{3,2,1,0:T(8,128)}, u32[]{:S(2)}, u32[]{:S(2)}) collective-permute-start(f32[3,1,16,128]{3,2,1,0:T(8,128)} %get-tuple-element.47), channel_id=1, source_target_pairs={{8,0},{16,8},{24,16},{9,1},{17,9},{25,17},{10,2},{18,10},{26,18},{... | collective-permute-start | bytes 73736 | tf_op jit(solution)/shard_map/ppermute | solution.py:14
  587.0 13.6 %collective-permute-start.93 = (f32[3,32,1,128]{3,2,1,0:T(1,128)}, f32[3,32,1,128]{3,2,1,0:T(1,128)S(1)}, u32[]{:S(2)}, u32[]{:S(2)}) collective-permute-start(f32[3,32,1,128]{3,2,1,0:T(1,128)} %get-tuple-element.42), channel_id=1, source_target_pairs={{0,2},{2,4},{4,6},{1,3},{3,5},{5,7},{8,10},{10,12},{12,14},{9,11},... | collective-permute-start | bytes 147464 | tf_op jit(solution)/shard_map/ppermute | solution.py:14
  604.5 13.8 %collective-permute-start.96 = (f32[1,16,128]{2,1,0:T(8,128)S(1)}, f32[1,16,128]{2,1,0:T(8,128)S(1)}, u32[]{:S(2)}, u32[]{:S(2)}) collective-permute-start(f32[1,16,128]{2,1,0:T(8,128)S(1)} %slice_bitcast_fusion.16), channel_id=1, source_target_pairs={{0,8},{8,16},{16,24},{1,9},{9,17},{17,25},{2,10},{10,18},{18,26},{... | collective-permute-start | bytes 24584 | tf_op jit(solution)/shard_map/ppermute | solution.py:14
  609.2 9.1 %collective-permute-start.97 = (f32[32,1,128]{2,1,0:T(1,128)S(1)}, f32[32,1,128]{2,1,0:T(1,128)S(1)}, u32[]{:S(2)}, u32[]{:S(2)}) collective-permute-start(f32[32,1,128]{2,1,0:T(1,128)S(1)} %slice.1226), channel_id=1, source_target_pairs={{0,2},{2,4},{4,6},{1,3},{3,5},{5,7},{8,10},{10,12},{12,14},{9,11},... | collective-permute-start | bytes 49160 | tf_op jit(solution)/shard_map/ppermute | solution.py:14
  (107 other events, 689.1 us)
where the time goes:
time: 679 us; the launch traced here: 667 us
  starting transfers between devices  274 us (40%)
  local copies, waits for them, and re-layouts  165 us (24%)
  blocking collectives  130 us (19%)
  other arithmetic  64.1 us (9%)
  between operations  21.6 us (3%)
  waiting for transfers between devices  12.4 us (2%)
    ppermute x93, starting transfers between devices, passed_along(): return lax.ppermute(value, axis, pairs)  259 us
    psum x3, blocking collectives, per_device(): lax.psum((jnp.sum(residual * scaled), jnp.sum(applied * scaled), jnp.sum(...  130 us
    slice x48, local copies, waits for them, and re-layouts, viscous(): tail = lax.slice_in_dim(state, length - 1, length, axis=dim)  52.2 us
    add x12, other arithmetic, sweeps(): state = state + OMEGA * inverse * (source - viscous(state, faces, diag))  48.6 us
    slice x36, local copies, waits for them, and re-layouts, viscous(): lax.slice_in_dim(state, 0, length - 1, axis=dim)  48.5 us
    ppermute x24, local copies, waits for them, and re-layouts, passed_along(): return lax.ppermute(value, axis, pairs)  42.5 us
  transfers between devices with their start and end apart: 99, of which 8 were waited for; matrix products, arithmetic and copies ran while one was open for 12% of the time, Pallas kernels for 0%

commit v1 on v0

--- a/solution.py
+++ b/solution.py
@@ -2,10 +2,17 @@
 import jax.numpy as jnp
 from jax import lax
 from jax.sharding import PartitionSpec as P
+from jax.lax import psum
 
 ITERS = 3
 SWEEPS = 4
 OMEGA = 0.8
+
+
+def extend_the_meshes(mat):
+    extra = psum(mat, ("gy", "gz"))
+    current_value = psum(extra, "gx")
+    return current_value
 
 
 def passed_along(value, axis, by):
@@ -148,9 +155,8 @@
     applied = schur(scaled)
     for step in range(ITERS):
         last = step + 1 == ITERS
-        gamma, delta, squares = lax.psum(
-            (jnp.sum(residual * scaled), jnp.sum(applied * scaled), jnp.sum(residual * residual)),
-            ("gx", "gy", "gz"),
+        gamma, delta, squares = extend_the_meshes(
+            (jnp.sum(residual * scaled), jnp.sum(applied * scaled), jnp.sum(residual * residual))
         )
         norms.append(squares / cells)
         if not last:

time: 679 us -> 626 us (0.922)
  blocking collectives: 130 us -> 84.1 us
    psum x3 -> x6, blocking collectives: 130 us -> 84.1 us  [the longest x3 49.8 us: extend_the_meshes(): extra = psum(mat, ('gy', 'gz'))]
  transfers between devices with their start and end apart: 99 -> 99, of which waited for: 8 -> 8; matrix products, arithmetic and copies ran while one was open for 12% -> 13% of each run, Pallas kernels for 0% -> 0%
where the time goes in v1:
time: 626 us; the launch traced here: 615 us
  starting transfers between devices  268 us (43%)
  local copies, waits for them, and re-layouts  164 us (26%)
  blocking collectives  84.1 us (13%)
  other arithmetic  64.2 us (10%)
  between operations  22 us (4%)
  waiting for transfers between devices  12.4 us (2%)
    ppermute x93, starting transfers between devices, passed_along(): return lax.ppermute(value, axis, pairs)  253 us
    slice x48, local copies, waits for them, and re-layouts, viscous(): tail = lax.slice_in_dim(state, length - 1, length, axis=dim)  51.9 us
    psum x3, blocking collectives, extend_the_meshes(): extra = psum(mat, ('gy', 'gz'))  49.8 us
    slice x36, local copies, waits for them, and re-layouts, viscous(): lax.slice_in_dim(state, 0, length - 1, axis=dim)  48.7 us
    add x12, other arithmetic, sweeps(): state = state + OMEGA * inverse * (source - viscous(state, faces, diag))  48.5 us
    ppermute x24, local copies, waits for them, and re-layouts, passed_along(): return lax.ppermute(value, axis, pairs)  41.7 us
    psum x3, blocking collectives, extend_the_meshes(): current_value = psum(extra, 'gx')  34.2 us
  transfers between devices with their start and end apart: 99, of which 8 were waited for; matrix products, arithmetic and copies ran while one was open for 13% of the time, Pallas kernels for 0%

profile of v1, /device:TPU:0, one launch (start us, length us, event | category | flops | bytes accessed | tf_op | source)
XLA Modules:
  0.0 614.6 jit_solution(1503515150353310363)
XLA Ops:
  2.6 5.5 collective-permute-start
  10.5 4.0 collective-permute-start.2
  16.5 3.6 collective-permute-done.3
  31.0 6.0 select_add_fusion
  46.9 3.0 collective-permute-start.11
  50.6 4.3 collective-permute-start.7
  56.2 3.5 collective-permute-start.9
  67.9 4.1 fusion.8
  78.6 3.6 collective-permute-start.17
  82.9 6.3 %collective-permute-start.13 = (f32[3,1,16,128]{3,2,1,0:T(8,128)}, f32[3,1,16,128]{3,2,1,0:T(8,128)}, u32[]{:S(2)}, u32[]{:S(2)}) collective-permute-start(f32[3,1,16,128]{3,2,1,0:T(8,128)} %get-tuple-element.181), channel_id=1, source_target_pairs={{0,8},{8,16},{16,24},{1,9},{9,17},{17,25},{2,10},{10,18},{18,26},{... | collective-permute-start | bytes 73736 | tf_op jit(solution)/shard_map/ppermute | solution.py:21
  90.5 4.5 collective-permute-start.15
  103.4 4.2 fusion.17
  114.3 3.6 collective-permute-start.23
  118.5 5.5 collective-permute-start.19
  125.3 4.5 collective-permute-start.21
  138.9 4.0 fusion.26
  142.9 4.9 collective-permute-start.24
  147.8 4.5 collective-permute-start.25
  152.5 3.1 collective-permute-start.26
  175.8 5.3 collective-permute-start.31
  182.4 4.5 collective-permute-start.33
  196.0 4.1 fusion.35
  206.8 4.2 collective-permute-start.41
  211.6 5.1 collective-permute-start.37
  218.0 4.5 collective-permute-start.39
  231.0 4.2 fusion.44
  241.9 3.6 collective-permute-start.47
  246.2 5.5 collective-permute-start.43
  252.9 4.5 collective-permute-start.45
  266.5 4.0 fusion.53
  270.5 4.9 collective-permute-start.48
  275.4 4.5 collective-permute-start.49
  280.1 3.2 collective-permute-start.50
  290.1 18.4 %all-reduce.2 = (f32[]{:T(128)}, f32[]{:T(128)}) all-reduce(f32[]{:T(128)} %get-tuple-element.14, f32[]{:T(128)} %get-tuple-element.13), channel_id=1, replica_groups=mesh['gx'=4,'gy'=4,'gz'=2] {'gy','gz'}, use_global_device_ids=true, to_apply=%region_1.2 | all-reduce | flops 2 | bytes 16 | tf_op jit(solution)/shard_map/psum | solution.py:13
  308.5 12.0 %all-reduce.5 = (f32[]{:T(128)}, f32[]{:T(128)}) all-reduce(f32[]{:T(128)} %get-tuple-element.22, f32[]{:T(128)} %get-tuple-element.23), channel_id=1, replica_groups=mesh['gx'=4,'gy'=4,'gz'=2] {'gx'}, use_global_device_ids=true, to_apply=%region_2.3 | all-reduce | flops 2 | bytes 16 | tf_op jit(solution)/shard_map/psum | solution.py:14
  332.3 4.2 collective-permute-start.55
  348.2 4.1 fusion.62
  358.9 4.2 collective-permute-start.65
  363.7 5.1 collective-permute-start.61
  370.2 4.5 collective-permute-start.63
  383.3 4.2 fusion.71
  394.2 3.6 collective-permute-start.71
  398.5 5.1 collective-permute-start.67
  404.9 4.5 collective-permute-start.69
  418.5 4.0 fusion.80
  422.5 4.7 collective-permute-start.72
  427.3 4.5 collective-permute-start.73
  432.0 3.2 collective-permute-start.74
  442.0 16.7 %all-reduce.1 = (f32[]{:T(128)}, f32[]{:T(128)}) all-reduce(f32[]{:T(128)} %get-tuple-element.9, f32[]{:T(128)} %get-tuple-element.8), channel_id=1, replica_groups=mesh['gx'=4,'gy'=4,'gz'=2] {'gy','gz'}, use_global_device_ids=true, to_apply=%region_7.8 | all-reduce | flops 2 | bytes 16 | tf_op jit(solution)/shard_map/psum | solution.py:13
  458.7 11.6 %all-reduce.4 = (f32[]{:T(128)}, f32[]{:T(128)}) all-reduce(f32[]{:T(128)} %get-tuple-element.20, f32[]{:T(128)} %get-tuple-element.21), channel_id=1, replica_groups=mesh['gx'=4,'gy'=4,'gz'=2] {'gx'}, use_global_device_ids=true, to_apply=%region_8.9 | all-reduce | flops 2 | bytes 16 | tf_op jit(solution)/shard_map/psum | solution.py:14
  484.2 3.9 collective-permute-start.79
  498.2 3.8 fusion.89
  510.6 4.5 collective-permute-start.85
  516.4 4.5 collective-permute-start.87
  528.0 4.0 fusion.98
  538.7 3.6 collective-permute-start.95
  543.0 5.1 collective-permute-start.91
  549.4 4.5 collective-permute-start.93
  563.0 3.8 fusion.107
  566.9 4.7 collective-permute-start.96
  571.6 4.5 collective-permute-start.97
  576.3 3.2 collective-permute-start.98
  581.7 14.7 %all-reduce = (f32[]{:T(128)}, f32[]{:T(128)}, f32[]{:T(128)}, f32[]{:T(128)}, f32[]{:T(128)}) all-reduce(f32[]{:T(128)} %get-tuple-element.7, f32[]{:T(128)} %get-tuple-element.12, f32[]{:T(128)} %get-tuple-element.6, f32[]{:T(128)} %get-tuple-element.10, f32[]{:T(128)} %get-tuple-element.11), channel_id=1, replica_groups=mesh['gx'=4,'gy'=4,'gz'=2] {'gy','gz'}, use_global_device_ids=true, to_apply=%region_13.14 | all-reduce | flops 5 | bytes 40 | tf_op jit(solution)/shard_map/psum | solution.py:13
  596.3 10.6 %all-reduce.3 = (f32[]{:T(128)}, f32[]{:T(128)}, f32[]{:T(128)}, f32[]{:T(128)}, f32[]{:T(128)}) all-reduce(f32[]{:T(128)} %get-tuple-element.15, f32[]{:T(128)} %get-tuple-element.16, f32[]{:T(128)} %get-tuple-element.17, f32[]{:T(128)} %get-tuple-element.18, f32[]{:T(128)} %get-tuple-element.19), channel_id=1, replica_groups=mesh['gx'=4,'gy'=4,'gz'=2] {'gx'}, use_global_device_ids=true, to_apply=%region_14.15 | all-reduce | flops 5 | bytes 40 | tf_op jit(solution)/shard_map/psum | solution.py:14
  (487 shorter events, 256.9 us)
Async XLA Ops:
  1.3 9.1 %collective-permute-start.1 = (s32[1,16,128]{2,1,0:T(8,128)S(1)}, s32[1,16,128]{2,1,0:T(8,128)S(1)}, u32[]{:S(2)}, u32[]{:S(2)}) collective-permute-start(s32[1,16,128]{2,1,0:T(8,128)S(1)} %get-tuple-element.210), channel_id=1, source_target_pairs={{8,0},{16,8},{24,16},{9,1},{17,9},{25,17},{10,2},{18,10},{26,18},{... | collective-permute-start | bytes 24584 | tf_op jit(solution)/shard_map/ppermute | solution.py:34
  20.4 10.6 %collective-permute-start.4 = (s32[34,18,1]{2,1,0:T(8,128)S(1)}, s32[34,18,1]{2,1,0:T(8,128)S(1)}, u32[]{:S(2)}, u32[]{:S(2)}) collective-permute-start(s32[34,18,1]{2,1,0:T(8,128)S(1)} %get-tuple-element.197), channel_id=1, source_target_pairs={{0,1},{2,3},{4,5},{6,7},{8,9},{10,11},{12,13},{14,15},{16,17},{18,... | collective-permute-start | bytes 7352 | tf_op jit(solution)/shard_map/ppermute | solution.py:32
  21.8 9.3 %collective-permute-start.5 = (s32[34,18,1]{2,1,0:T(8,128)S(1)}, s32[34,18,1]{2,1,0:T(8,128)S(1)}, u32[]{:S(2)}, u32[]{:S(2)}) collective-permute-start(s32[34,18,1]{2,1,0:T(8,128)S(1)} %get-tuple-element.198), channel_id=1, source_target_pairs={{1,0},{3,2},{5,4},{7,6},{9,8},{11,10},{13,12},{15,14},{17,16},{19,... | collective-permute-start | bytes 7352 | tf_op jit(solution)/shard_map/ppermute | solution.py:34
  46.9 14.5 %collective-permute-start.11 = (f32[3,32,16,1]{1,2,3,0:T(8,128)S(1)}, f32[3,32,16,1]{1,2,3,0:T(8,128)S(1)}, u32[]{:S(2)}, u32[]{:S(2)}) collective-permute-start(f32[3,32,16,1]{1,2,3,0:T(8,128)S(1)} %copy.22), channel_id=1, source_target_pairs={{0,1},{2,3},{4,5},{6,7},{8,9},{10,11},{12,13},{14,15},{16,17},{18,... | collective-permute-start | bytes 18440 | tf_op jit(solution)/shard_map/ppermute | solution.py:21
  50.6 16.7 %collective-permute-start.7 = (f32[3,1,16,128]{3,2,1,0:T(8,128)}, f32[3,1,16,128]{3,2,1,0:T(8,128)S(1)}, u32[]{:S(2)}, u32[]{:S(2)}) collective-permute-start(f32[3,1,16,128]{3,2,1,0:T(8,128)} %get-tuple-element.193), channel_id=1, source_target_pairs={{0,8},{8,16},{16,24},{1,9},{9,17},{17,25},{2,10},{10,18},{18,26},{... | collective-permute-start | bytes 73736 | tf_op jit(solution)/shard_map/ppermute | solution.py:21
  54.9 12.4 %collective-permute-start.6 = (f32[3,1,16,128]{3,2,1,0:T(8,128)}, f32[3,1,16,128]{3,2,1,0:T(8,128)S(1)}, u32[]{:S(2)}, u32[]{:S(2)}) collective-permute-start(f32[3,1,16,128]{3,2,1,0:T(8,128)} %get-tuple-element.194), channel_id=1, source_target_pairs={{8,0},{16,8},{24,16},{9,1},{17,9},{25,17},{10,2},{18,10},{26,18},{... | collective-permute-start | bytes 73736 | tf_op jit(solution)/shard_map/ppermute | solution.py:21
  56.2 11.1 %collective-permute-start.9 = (f32[3,32,1,128]{3,2,1,0:T(1,128)}, f32[3,32,1,128]{3,2,1,0:T(1,128)S(1)}, u32[]{:S(2)}, u32[]{:S(2)}) collective-permute-start(f32[3,32,1,128]{3,2,1,0:T(1,128)} %get-tuple-element.189), channel_id=1, source_target_pairs={{0,2},{2,4},{4,6},{1,3},{3,5},{5,7},{8,10},{10,12},{12,14},{9,11},... | collective-permute-start | bytes 147464 | tf_op jit(solution)/shard_map/ppermute | solution.py:21
  78.6 18.7 %collective-permute-start.17 = (f32[3,32,16,1]{1,2,3,0:T(8,128)}, f32[3,32,16,1]{1,2,3,0:T(8,128)}, u32[]{:S(2)}, u32[]{:S(2)}) collective-permute-start(f32[3,32,16,1]{1,2,3,0:T(8,128)} %copy.26), channel_id=1, source_target_pairs={{0,1},{2,3},{4,5},{6,7},{8,9},{10,11},{12,13},{14,15},{16,17},{18,... | collective-permute-start | bytes 18440 | tf_op jit(solution)/shard_map/ppermute | solution.py:21
  82.9 20.5 %collective-permute-start.13 = (f32[3,1,16,128]{3,2,1,0:T(8,128)}, f32[3,1,16,128]{3,2,1,0:T(8,128)}, u32[]{:S(2)}, u32[]{:S(2)}) collective-permute-start(f32[3,1,16,128]{3,2,1,0:T(8,128)} %get-tuple-element.181), channel_id=1, source_target_pairs={{0,8},{8,16},{16,24},{1,9},{9,17},{17,25},{2,10},{10,18},{18,26},{... | collective-permute-start | bytes 73736 | tf_op jit(solution)/shard_map/ppermute | solution.py:21
  89.2 14.2 %collective-permute-start.12 = (f32[3,1,16,128]{3,2,1,0:T(8,128)}, f32[3,1,16,128]{3,2,1,0:T(8,128)}, u32[]{:S(2)}, u32[]{:S(2)}) collective-permute-start(f32[3,1,16,128]{3,2,1,0:T(8,128)} %get-tuple-element.182), channel_id=1, source_target_pairs={{8,0},{16,8},{24,16},{9,1},{17,9},{25,17},{10,2},{18,10},{26,18},{... | collective-permute-start | bytes 73736 | tf_op jit(solution)/shard_map/ppermute | solution.py:21
  90.5 12.9 %collective-permute-start.15 = (f32[3,32,1,128]{3,2,1,0:T(1,128)}, f32[3,32,1,128]{3,2,1,0:T(1,128)S(1)}, u32[]{:S(2)}, u32[]{:S(2)}) collective-permute-start(f32[3,32,1,128]{3,2,1,0:T(1,128)} %get-tuple-element.177), channel_id=1, source_target_pairs={{0,2},{2,4},{4,6},{1,3},{3,5},{5,7},{8,10},{10,12},{12,14},{9,11},... | collective-permute-start | bytes 147464 | tf_op jit(solution)/shard_map/ppermute | solution.py:21
  114.3 17.8 %collective-permute-start.23 = (f32[3,32,16,1]{1,2,3,0:T(8,128)}, f32[3,32,16,1]{1,2,3,0:T(8,128)}, u32[]{:S(2)}, u32[]{:S(2)}) collective-permute-start(f32[3,32,16,1]{1,2,3,0:T(8,128)} %copy.30), channel_id=1, source_target_pairs={{0,1},{2,3},{4,5},{6,7},{8,9},{10,11},{12,13},{14,15},{16,17},{18,... | collective-permute-start | bytes 18440 | tf_op jit(solution)/shard_map/ppermute | solution.py:21
  118.5 20.3 %collective-permute-start.19 = (f32[3,1,16,128]{3,2,1,0:T(8,128)}, f32[3,1,16,128]{3,2,1,0:T(8,128)}, u32[]{:S(2)}, u32[]{:S(2)}) collective-permute-start(f32[3,1,16,128]{3,2,1,0:T(8,128)} %get-tuple-element.169), channel_id=1, source_target_pairs={{0,8},{8,16},{16,24},{1,9},{9,17},{17,25},{2,10},{10,18},{18,26},{... | collective-permute-start | bytes 73736 | tf_op jit(solution)/shard_map/ppermute | solution.py:21
  124.0 14.8 %collective-permute-start.18 = (f32[3,1,16,128]{3,2,1,0:T(8,128)}, f32[3,1,16,128]{3,2,1,0:T(8,128)}, u32[]{:S(2)}, u32[]{:S(2)}) collective-permute-start(f32[3,1,16,128]{3,2,1,0:T(8,128)} %get-tuple-element.170), channel_id=1, source_target_pairs={{8,0},{16,8},{24,16},{9,1},{17,9},{25,17},{10,2},{18,10},{26,18},{... | collective-permute-start | bytes 73736 | tf_op jit(solution)/shard_map/ppermute | solution.py:21
  125.3 13.5 %collective-permute-start.21 = (f32[3,32,1,128]{3,2,1,0:T(1,128)}, f32[3,32,1,128]{3,2,1,0:T(1,128)S(1)}, u32[]{:S(2)}, u32[]{:S(2)}) collective-permute-start(f32[3,32,1,128]{3,2,1,0:T(1,128)} %get-tuple-element.165), channel_id=1, source_target_pairs={{0,2},{2,4},{4,6},{1,3},{3,5},{5,7},{8,10},{10,12},{12,14},{9,11},... | collective-permute-start | bytes 147464 | tf_op jit(solution)/shard_map/ppermute | solution.py:21
  142.9 13.8 %collective-permute-start.24 = (f32[1,16,128]{2,1,0:T(8,128)S(1)}, f32[1,16,128]{2,1,0:T(8,128)S(1)}, u32[]{:S(2)}, u32[]{:S(2)}) collective-permute-start(f32[1,16,128]{2,1,0:T(8,128)S(1)} %slice_bitcast_fusion.19), channel_id=1, source_target_pairs={{0,8},{8,16},{16,24},{1,9},{9,17},{17,25},{2,10},{10,18},{18,26},{... | collective-permute-start | bytes 24584 | tf_op jit(solution)/shard_map/ppermute | solution.py:21
  173.2 16.0 %collective-permute-start.35 = (f32[3,32,16,1]{1,2,3,0:T(8,128)}, f32[3,32,16,1]{1,2,3,0:T(8,128)}, u32[]{:S(2)}, u32[]{:S(2)}) collective-permute-start(f32[3,32,16,1]{1,2,3,0:T(8,128)} %copy.34), channel_id=1, source_target_pairs={{0,1},{2,3},{4,5},{6,7},{8,9},{10,11},{12,13},{14,15},{16,17},{18,... | collective-permute-start | bytes 18440 | tf_op jit(solution)/shard_map/ppermute | solution.py:21
  175.8 20.1 %collective-permute-start.31 = (f32[3,1,16,128]{3,2,1,0:T(8,128)}, f32[3,1,16,128]{3,2,1,0:T(8,128)}, u32[]{:S(2)}, u32[]{:S(2)}) collective-permute-start(f32[3,1,16,128]{3,2,1,0:T(8,128)} %get-tuple-element.155), channel_id=1, source_target_pairs={{0,8},{8,16},{16,24},{1,9},{9,17},{17,25},{2,10},{10,18},{18,26},{... | collective-permute-start | bytes 73736 | tf_op jit(solution)/shard_map/ppermute | solution.py:21
  181.1 14.8 %collective-permute-start.30 = (f32[3,1,16,128]{3,2,1,0:T(8,128)}, f32[3,1,16,128]{3,2,1,0:T(8,128)}, u32[]{:S(2)}, u32[]{:S(2)}) collective-permute-start(f32[3,1,16,128]{3,2,1,0:T(8,128)} %get-tuple-element.156), channel_id=1, source_target_pairs={{8,0},{16,8},{24,16},{9,1},{17,9},{25,17},{10,2},{18,10},{26,18},{... | collective-permute-start | bytes 73736 | tf_op jit(solution)/shard_map/ppermute | solution.py:21
  182.4 13.5 %collective-permute-start.33 = (f32[3,32,1,128]{3,2,1,0:T(1,128)}, f32[3,32,1,128]{3,2,1,0:T(1,128)S(1)}, u32[]{:S(2)}, u32[]{:S(2)}) collective-permute-start(f32[3,32,1,128]{3,2,1,0:T(1,128)} %get-tuple-element.151), channel_id=1, source_target_pairs={{0,2},{2,4},{4,6},{1,3},{3,5},{5,7},{8,10},{10,12},{12,14},{9,11},... | collective-permute-start | bytes 147464 | tf_op jit(solution)/shard_map/ppermute | solution.py:21
  206.8 18.1 %collective-permute-start.41 = (f32[3,32,16,1]{1,2,3,0:T(8,128)}, f32[3,32,16,1]{1,2,3,0:T(8,128)}, u32[]{:S(2)}, u32[]{:S(2)}) collective-permute-start(f32[3,32,16,1]{1,2,3,0:T(8,128)} %copy.38), channel_id=1, source_target_pairs={{0,1},{2,3},{4,5},{6,7},{8,9},{10,11},{12,13},{14,15},{16,17},{18,... | collective-permute-start | bytes 18440 | tf_op jit(solution)/shard_map/ppermute | solution.py:21
  211.6 19.4 %collective-permute-start.37 = (f32[3,1,16,128]{3,2,1,0:T(8,128)}, f32[3,1,16,128]{3,2,1,0:T(8,128)}, u32[]{:S(2)}, u32[]{:S(2)}) collective-permute-start(f32[3,1,16,128]{3,2,1,0:T(8,128)} %get-tuple-element.143), channel_id=1, source_target_pairs={{0,8},{8,16},{16,24},{1,9},{9,17},{17,25},{2,10},{10,18},{18,26},{... | collective-permute-start | bytes 73736 | tf_op jit(solution)/shard_map/ppermute | solution.py:21
  216.7 14.2 %collective-permute-start.36 = (f32[3,1,16,128]{3,2,1,0:T(8,128)}, f32[3,1,16,128]{3,2,1,0:T(8,128)}, u32[]{:S(2)}, u32[]{:S(2)}) collective-permute-start(f32[3,1,16,128]{3,2,1,0:T(8,128)} %get-tuple-element.144), channel_id=1, source_target_pairs={{8,0},{16,8},{24,16},{9,1},{17,9},{25,17},{10,2},{18,10},{26,18},{... | collective-permute-start | bytes 73736 | tf_op jit(solution)/shard_map/ppermute | solution.py:21
  218.0 12.9 %collective-permute-start.39 = (f32[3,32,1,128]{3,2,1,0:T(1,128)}, f32[3,32,1,128]{3,2,1,0:T(1,128)S(1)}, u32[]{:S(2)}, u32[]{:S(2)}) collective-permute-start(f32[3,32,1,128]{3,2,1,0:T(1,128)} %get-tuple-element.139), channel_id=1, source_target_pairs={{0,2},{2,4},{4,6},{1,3},{3,5},{5,7},{8,10},{10,12},{12,14},{9,11},... | collective-permute-start | bytes 147464 | tf_op jit(solution)/shard_map/ppermute | solution.py:21
  241.9 17.8 %collective-permute-start.47 = (f32[3,32,16,1]{1,2,3,0:T(8,128)}, f32[3,32,16,1]{1,2,3,0:T(8,128)}, u32[]{:S(2)}, u32[]{:S(2)}) collective-permute-start(f32[3,32,16,1]{1,2,3,0:T(8,128)} %copy.42), channel_id=1, source_target_pairs={{0,1},{2,3},{4,5},{6,7},{8,9},{10,11},{12,13},{14,15},{16,17},{18,... | collective-permute-start | bytes 18440 | tf_op jit(solution)/shard_map/ppermute | solution.py:21
  246.2 20.3 %collective-permute-start.43 = (f32[3,1,16,128]{3,2,1,0:T(8,128)}, f32[3,1,16,128]{3,2,1,0:T(8,128)}, u32[]{:S(2)}, u32[]{:S(2)}) collective-permute-start(f32[3,1,16,128]{3,2,1,0:T(8,128)} %get-tuple-element.131), channel_id=1, source_target_pairs={{0,8},{8,16},{16,24},{1,9},{9,17},{17,25},{2,10},{10,18},{18,26},{... | collective-permute-start | bytes 73736 | tf_op jit(solution)/shard_map/ppermute | solution.py:21
  251.6 14.8 %collective-permute-start.42 = (f32[3,1,16,128]{3,2,1,0:T(8,128)}, f32[3,1,16,128]{3,2,1,0:T(8,128)}, u32[]{:S(2)}, u32[]{:S(2)}) collective-permute-start(f32[3,1,16,128]{3,2,1,0:T(8,128)} %get-tuple-element.132), channel_id=1, source_target_pairs={{8,0},{16,8},{24,16},{9,1},{17,9},{25,17},{10,2},{18,10},{26,18},{... | collective-permute-start | bytes 73736 | tf_op jit(solution)/shard_map/ppermute | solution.py:21
  252.9 13.5 %collective-permute-start.45 = (f32[3,32,1,128]{3,2,1,0:T(1,128)}, f32[3,32,1,128]{3,2,1,0:T(1,128)S(1)}, u32[]{:S(2)}, u32[]{:S(2)}) collective-permute-start(f32[3,32,1,128]{3,2,1,0:T(1,128)} %get-tuple-element.127), channel_id=1, source_target_pairs={{0,2},{2,4},{4,6},{1,3},{3,5},{5,7},{8,10},{10,12},{12,14},{9,11},... | collective-permute-start | bytes 147464 | tf_op jit(solution)/shard_map/ppermute | solution.py:21
  270.5 14.0 %collective-permute-start.48 = (f32[1,16,128]{2,1,0:T(8,128)S(1)}, f32[1,16,128]{2,1,0:T(8,128)S(1)}, u32[]{:S(2)}, u32[]{:S(2)}) collective-permute-start(f32[1,16,128]{2,1,0:T(8,128)S(1)} %slice_bitcast_fusion.18), channel_id=1, source_target_pairs={{0,8},{8,16},{16,24},{1,9},{9,17},{17,25},{2,10},{10,18},{18,26},{... | collective-permute-start | bytes 24584 | tf_op jit(solution)/shard_map/ppermute | solution.py:21
  275.4 9.1 %collective-permute-start.49 = (f32[32,1,128]{2,1,0:T(1,128)S(1)}, f32[32,1,128]{2,1,0:T(1,128)S(1)}, u32[]{:S(2)}, u32[]{:S(2)}) collective-permute-start(f32[32,1,128]{2,1,0:T(1,128)S(1)} %slice.1124), channel_id=1, source_target_pairs={{0,2},{2,4},{4,6},{1,3},{3,5},{5,7},{8,10},{10,12},{12,14},{9,11},... | collective-permute-start | bytes 49160 | tf_op jit(solution)/shard_map/ppermute | solution.py:21
  286.1 35.9 %collective-permute-start.52 = (f32[32,1,128]{2,1,0:T(1,128)S(1)}, f32[32,1,128]{2,1,0:T(1,128)S(1)}, u32[]{:S(2)}, u32[]{:S(2)}) collective-permute-start(f32[32,1,128]{2,1,0:T(1,128)S(1)} %slice.1132), channel_id=1, source_target_pairs={{2,0},{4,2},{6,4},{3,1},{5,3},{7,5},{10,8},{12,10},{14,12},{11,9},... | collective-permute-start | bytes 49160 | tf_op jit(solution)/shard_map/ppermute | solution.py:21
  287.5 34.6 %collective-permute-start.51 = (f32[1,16,128]{2,1,0:T(8,128)S(1)}, f32[1,16,128]{2,1,0:T(8,128)S(1)}, u32[]{:S(2)}, u32[]{:S(2)}) collective-permute-start(f32[1,16,128]{2,1,0:T(8,128)S(1)} %slice.1130), channel_id=1, source_target_pairs={{8,0},{16,8},{24,16},{9,1},{17,9},{25,17},{10,2},{18,10},{26,18},{... | collective-permute-start | bytes 24584 | tf_op jit(solution)/shard_map/ppermute | solution.py:21
  288.8 33.3 %collective-permute-start.53 = (f32[32,16,1]{2,1,0:T(8,128)S(1)}, f32[32,16,1]{2,1,0:T(8,128)S(1)}, u32[]{:S(2)}, u32[]{:S(2)}) collective-permute-start(f32[32,16,1]{2,1,0:T(8,128)S(1)} %bitcast.173), channel_id=1, source_target_pairs={{1,0},{3,2},{5,4},{7,6},{9,8},{11,10},{13,12},{15,14},{17,16},{19,... | collective-permute-start | bytes 6152 | tf_op jit(solution)/shard_map/ppermute | solution.py:21
  329.8 11.6 %collective-permute-start.59 = (f32[3,32,16,1]{1,2,3,0:T(8,128)}, f32[3,32,16,1]{1,2,3,0:T(8,128)}, u32[]{:S(2)}, u32[]{:S(2)}) collective-permute-start(f32[3,32,16,1]{1,2,3,0:T(8,128)} %copy.46), channel_id=1, source_target_pairs={{0,1},{2,3},{4,5},{6,7},{8,9},{10,11},{12,13},{14,15},{16,17},{18,... | collective-permute-start | bytes 18440 | tf_op jit(solution)/shard_map/ppermute | solution.py:21
  332.3 15.8 %collective-permute-start.55 = (f32[3,1,16,128]{3,2,1,0:T(8,128)}, f32[3,1,16,128]{3,2,1,0:T(8,128)}, u32[]{:S(2)}, u32[]{:S(2)}) collective-permute-start(f32[3,1,16,128]{3,2,1,0:T(8,128)} %get-tuple-element.117), channel_id=1, source_target_pairs={{0,8},{8,16},{16,24},{1,9},{9,17},{17,25},{2,10},{10,18},{18,26},{... | collective-permute-start | bytes 73736 | tf_op jit(solution)/shard_map/ppermute | solution.py:21
  336.5 11.6 %collective-permute-start.54 = (f32[3,1,16,128]{3,2,1,0:T(8,128)}, f32[3,1,16,128]{3,2,1,0:T(8,128)}, u32[]{:S(2)}, u32[]{:S(2)}) collective-permute-start(f32[3,1,16,128]{3,2,1,0:T(8,128)} %get-tuple-element.118), channel_id=1, source_target_pairs={{8,0},{16,8},{24,16},{9,1},{17,9},{25,17},{10,2},{18,10},{26,18},{... | collective-permute-start | bytes 73736 | tf_op jit(solution)/shard_map/ppermute | solution.py:21
  337.8 10.3 %collective-permute-start.57 = (f32[3,32,1,128]{3,2,1,0:T(1,128)}, f32[3,32,1,128]{3,2,1,0:T(1,128)S(1)}, u32[]{:S(2)}, u32[]{:S(2)}) collective-permute-start(f32[3,32,1,128]{3,2,1,0:T(1,128)} %get-tuple-element.113), channel_id=1, source_target_pairs={{0,2},{2,4},{4,6},{1,3},{3,5},{5,7},{8,10},{10,12},{12,14},{9,11},... | collective-permute-start | bytes 147464 | tf_op jit(solution)/shard_map/ppermute | solution.py:21
  358.9 18.1 %collective-permute-start.65 = (f32[3,32,16,1]{1,2,3,0:T(8,128)}, f32[3,32,16,1]{1,2,3,0:T(8,128)}, u32[]{:S(2)}, u32[]{:S(2)}) collective-permute-start(f32[3,32,16,1]{1,2,3,0:T(8,128)} %copy.50), channel_id=1, source_target_pairs={{0,1},{2,3},{4,5},{6,7},{8,9},{10,11},{12,13},{14,15},{16,17},{18,... | collective-permute-start | bytes 18440 | tf_op jit(solution)/shard_map/ppermute | solution.py:21
  363.7 19.5 %collective-permute-start.61 = (f32[3,1,16,128]{3,2,1,0:T(8,128)}, f32[3,1,16,128]{3,2,1,0:T(8,128)}, u32[]{:S(2)}, u32[]{:S(2)}) collective-permute-start(f32[3,1,16,128]{3,2,1,0:T(8,128)} %get-tuple-element.105), channel_id=1, source_target_pairs={{0,8},{8,16},{16,24},{1,9},{9,17},{17,25},{2,10},{10,18},{18,26},{... | collective-permute-start | bytes 73736 | tf_op jit(solution)/shard_map/ppermute | solution.py:21
  368.9 14.4 %collective-permute-start.60 = (f32[3,1,16,128]{3,2,1,0:T(8,128)}, f32[3,1,16,128]{3,2,1,0:T(8,128)}, u32[]{:S(2)}, u32[]{:S(2)}) collective-permute-start(f32[3,1,16,128]{3,2,1,0:T(8,128)} %get-tuple-element.106), channel_id=1, source_target_pairs={{8,0},{16,8},{24,16},{9,1},{17,9},{25,17},{10,2},{18,10},{26,18},{... | collective-permute-start | bytes 73736 | tf_op jit(solution)/shard_map/ppermute | solution.py:21
  370.2 13.1 %collective-permute-start.63 = (f32[3,32,1,128]{3,2,1,0:T(1,128)}, f32[3,32,1,128]{3,2,1,0:T(1,128)S(1)}, u32[]{:S(2)}, u32[]{:S(2)}) collective-permute-start(f32[3,32,1,128]{3,2,1,0:T(1,128)} %get-tuple-element.101), channel_id=1, source_target_pairs={{0,2},{2,4},{4,6},{1,3},{3,5},{5,7},{8,10},{10,12},{12,14},{9,11},... | collective-permute-start | bytes 147464 | tf_op jit(solution)/shard_map/ppermute | solution.py:21
  394.2 17.5 %collective-permute-start.71 = (f32[3,32,16,1]{1,2,3,0:T(8,128)}, f32[3,32,16,1]{1,2,3,0:T(8,128)}, u32[]{:S(2)}, u32[]{:S(2)}) collective-permute-start(f32[3,32,16,1]{1,2,3,0:T(8,128)} %copy.54), channel_id=1, source_target_pairs={{0,1},{2,3},{4,5},{6,7},{8,9},{10,11},{12,13},{14,15},{16,17},{18,... | collective-permute-start | bytes 18440 | tf_op jit(solution)/shard_map/ppermute | solution.py:21
  398.5 20.0 %collective-permute-start.67 = (f32[3,1,16,128]{3,2,1,0:T(8,128)}, f32[3,1,16,128]{3,2,1,0:T(8,128)}, u32[]{:S(2)}, u32[]{:S(2)}) collective-permute-start(f32[3,1,16,128]{3,2,1,0:T(8,128)} %get-tuple-element.93), channel_id=1, source_target_pairs={{0,8},{8,16},{16,24},{1,9},{9,17},{17,25},{2,10},{10,18},{18,26},{... | collective-permute-start | bytes 73736 | tf_op jit(solution)/shard_map/ppermute | solution.py:21
  403.6 14.8 %collective-permute-start.66 = (f32[3,1,16,128]{3,2,1,0:T(8,128)}, f32[3,1,16,128]{3,2,1,0:T(8,128)}, u32[]{:S(2)}, u32[]{:S(2)}) collective-permute-start(f32[3,1,16,128]{3,2,1,0:T(8,128)} %get-tuple-element.94), channel_id=1, source_target_pairs={{8,0},{16,8},{24,16},{9,1},{17,9},{25,17},{10,2},{18,10},{26,18},{... | collective-permute-start | bytes 73736 | tf_op jit(solution)/shard_map/ppermute | solution.py:21
  404.9 13.5 %collective-permute-start.69 = (f32[3,32,1,128]{3,2,1,0:T(1,128)}, f32[3,32,1,128]{3,2,1,0:T(1,128)S(1)}, u32[]{:S(2)}, u32[]{:S(2)}) collective-permute-start(f32[3,32,1,128]{3,2,1,0:T(1,128)} %get-tuple-element.89), channel_id=1, source_target_pairs={{0,2},{2,4},{4,6},{1,3},{3,5},{5,7},{8,10},{10,12},{12,14},{9,11},... | collective-permute-start | bytes 147464 | tf_op jit(solution)/shard_map/ppermute | solution.py:21
  422.5 13.8 %collective-permute-start.72 = (f32[1,16,128]{2,1,0:T(8,128)S(1)}, f32[1,16,128]{2,1,0:T(8,128)S(1)}, u32[]{:S(2)}, u32[]{:S(2)}) collective-permute-start(f32[1,16,128]{2,1,0:T(8,128)S(1)} %slice_bitcast_fusion.17), channel_id=1, source_target_pairs={{0,8},{8,16},{16,24},{1,9},{9,17},{17,25},{2,10},{10,18},{18,26},{... | collective-permute-start | bytes 24584 | tf_op jit(solution)/shard_map/ppermute | solution.py:21
  427.3 9.1 %collective-permute-start.73 = (f32[32,1,128]{2,1,0:T(1,128)S(1)}, f32[32,1,128]{2,1,0:T(1,128)S(1)}, u32[]{:S(2)}, u32[]{:S(2)}) collective-permute-start(f32[32,1,128]{2,1,0:T(1,128)S(1)} %slice.1175), channel_id=1, source_target_pairs={{0,2},{2,4},{4,6},{1,3},{3,5},{5,7},{8,10},{10,12},{12,14},{9,11},... | collective-permute-start | bytes 49160 | tf_op jit(solution)/shard_map/ppermute | solution.py:21
  438.0 37.1 %collective-permute-start.76 = (f32[32,1,128]{2,1,0:T(1,128)S(1)}, f32[32,1,128]{2,1,0:T(1,128)S(1)}, u32[]{:S(2)}, u32[]{:S(2)}) collective-permute-start(f32[32,1,128]{2,1,0:T(1,128)S(1)} %slice.1183), channel_id=1, source_target_pairs={{2,0},{4,2},{6,4},{3,1},{5,3},{7,5},{10,8},{12,10},{14,12},{11,9},... | collective-permute-start | bytes 49160 | tf_op jit(solution)/shard_map/ppermute | solution.py:21
  439.4 35.8 %collective-permute-start.75 = (f32[1,16,128]{2,1,0:T(8,128)S(1)}, f32[1,16,128]{2,1,0:T(8,128)S(1)}, u32[]{:S(2)}, u32[]{:S(2)}) collective-permute-start(f32[1,16,128]{2,1,0:T(8,128)S(1)} %slice.1181), channel_id=1, source_target_pairs={{8,0},{16,8},{24,16},{9,1},{17,9},{25,17},{10,2},{18,10},{26,18},{... | collective-permute-start | bytes 24584 | tf_op jit(solution)/shard_map/ppermute | solution.py:21
  440.7 34.5 %collective-permute-start.77 = (f32[32,16,1]{2,1,0:T(8,128)S(1)}, f32[32,16,1]{2,1,0:T(8,128)S(1)}, u32[]{:S(2)}, u32[]{:S(2)}) collective-permute-start(f32[32,16,1]{2,1,0:T(8,128)S(1)} %bitcast.174), channel_id=1, source_target_pairs={{1,0},{3,2},{5,4},{7,6},{9,8},{11,10},{13,12},{15,14},{17,16},{19,... | collective-permute-start | bytes 6152 | tf_op jit(solution)/shard_map/ppermute | solution.py:21
  482.3 10.6 %collective-permute-start.83 = (f32[3,32,16,1]{1,2,3,0:T(8,128)S(1)}, f32[3,32,16,1]{1,2,3,0:T(8,128)S(1)}, u32[]{:S(2)}, u32[]{:S(2)}) collective-permute-start(f32[3,32,16,1]{1,2,3,0:T(8,128)S(1)} %copy.58), channel_id=1, source_target_pairs={{0,1},{2,3},{4,5},{6,7},{8,9},{10,11},{12,13},{14,15},{16,17},{18,... | collective-permute-start | bytes 18440 | tf_op jit(solution)/shard_map/ppermute | solution.py:21
  484.2 13.9 %collective-permute-start.79 = (f32[3,1,16,128]{3,2,1,0:T(8,128)}, f32[3,1,16,128]{3,2,1,0:T(8,128)}, u32[]{:S(2)}, u32[]{:S(2)}) collective-permute-start(f32[3,1,16,128]{3,2,1,0:T(8,128)} %get-tuple-element.79), channel_id=1, source_target_pairs={{0,8},{8,16},{16,24},{1,9},{9,17},{17,25},{2,10},{10,18},{18,26},{... | collective-permute-start | bytes 73736 | tf_op jit(solution)/shard_map/ppermute | solution.py:21
  488.1 10.0 %collective-permute-start.78 = (f32[3,1,16,128]{3,2,1,0:T(8,128)}, f32[3,1,16,128]{3,2,1,0:T(8,128)}, u32[]{:S(2)}, u32[]{:S(2)}) collective-permute-start(f32[3,1,16,128]{3,2,1,0:T(8,128)} %get-tuple-element.80), channel_id=1, source_target_pairs={{8,0},{16,8},{24,16},{9,1},{17,9},{25,17},{10,2},{18,10},{26,18},{... | collective-permute-start | bytes 73736 | tf_op jit(solution)/shard_map/ppermute | solution.py:21
  507.5 15.1 %collective-permute-start.89 = (f32[3,32,16,1]{1,2,3,0:T(8,128)S(1)}, f32[3,32,16,1]{1,2,3,0:T(8,128)S(1)}, u32[]{:S(2)}, u32[]{:S(2)}) collective-permute-start(f32[3,32,16,1]{1,2,3,0:T(8,128)S(1)} %copy.62), channel_id=1, source_target_pairs={{0,1},{2,3},{4,5},{6,7},{8,9},{10,11},{12,13},{14,15},{16,17},{18,... | collective-permute-start | bytes 18440 | tf_op jit(solution)/shard_map/ppermute | solution.py:21
  510.6 17.4 %collective-permute-start.85 = (f32[3,1,16,128]{3,2,1,0:T(8,128)S(1)}, f32[3,1,16,128]{3,2,1,0:T(8,128)S(1)}, u32[]{:S(2)}, u32[]{:S(2)}) collective-permute-start(f32[3,1,16,128]{3,2,1,0:T(8,128)S(1)} %get-tuple-element.67), channel_id=1, source_target_pairs={{0,8},{8,16},{16,24},{1,9},{9,17},{17,25},{2,10},{10,18},{18,26},{... | collective-permute-start | bytes 73736 | tf_op jit(solution)/shard_map/ppermute | solution.py:21
  515.1 12.9 %collective-permute-start.84 = (f32[3,1,16,128]{3,2,1,0:T(8,128)S(1)}, f32[3,1,16,128]{3,2,1,0:T(8,128)S(1)}, u32[]{:S(2)}, u32[]{:S(2)}) collective-permute-start(f32[3,1,16,128]{3,2,1,0:T(8,128)S(1)} %get-tuple-element.68), channel_id=1, source_target_pairs={{8,0},{16,8},{24,16},{9,1},{17,9},{25,17},{10,2},{18,10},{26,18},{... | collective-permute-start | bytes 73736 | tf_op jit(solution)/shard_map/ppermute | solution.py:21
  516.4 11.6 %collective-permute-start.87 = (f32[3,32,1,128]{3,2,1,0:T(1,128)S(1)}, f32[3,32,1,128]{3,2,1,0:T(1,128)S(1)}, u32[]{:S(2)}, u32[]{:S(2)}) collective-permute-start(f32[3,32,1,128]{3,2,1,0:T(1,128)S(1)} %get-tuple-element.63), channel_id=1, source_target_pairs={{0,2},{2,4},{4,6},{1,3},{3,5},{5,7},{8,10},{10,12},{12,14},{9,11},... | collective-permute-start | bytes 147464 | tf_op jit(solution)/shard_map/ppermute | solution.py:21
  538.7 17.5 %collective-permute-start.95 = (f32[3,32,16,1]{1,2,3,0:T(8,128)}, f32[3,32,16,1]{1,2,3,0:T(8,128)}, u32[]{:S(2)}, u32[]{:S(2)}) collective-permute-start(f32[3,32,16,1]{1,2,3,0:T(8,128)} %copy.66), channel_id=1, source_target_pairs={{0,1},{2,3},{4,5},{6,7},{8,9},{10,11},{12,13},{14,15},{16,17},{18,... | collective-permute-start | bytes 18440 | tf_op jit(solution)/shard_map/ppermute | solution.py:21
  543.0 20.0 %collective-permute-start.91 = (f32[3,1,16,128]{3,2,1,0:T(8,128)}, f32[3,1,16,128]{3,2,1,0:T(8,128)}, u32[]{:S(2)}, u32[]{:S(2)}) collective-permute-start(f32[3,1,16,128]{3,2,1,0:T(8,128)} %get-tuple-element.55), channel_id=1, source_target_pairs={{0,8},{8,16},{16,24},{1,9},{9,17},{17,25},{2,10},{10,18},{18,26},{... | collective-permute-start | bytes 73736 | tf_op jit(solution)/shard_map/ppermute | solution.py:21
  548.1 14.8 %collective-permute-start.90 = (f32[3,1,16,128]{3,2,1,0:T(8,128)}, f32[3,1,16,128]{3,2,1,0:T(8,128)}, u32[]{:S(2)}, u32[]{:S(2)}) collective-permute-start(f32[3,1,16,128]{3,2,1,0:T(8,128)} %get-tuple-element.56), channel_id=1, source_target_pairs={{8,0},{16,8},{24,16},{9,1},{17,9},{25,17},{10,2},{18,10},{26,18},{... | collective-permute-start | bytes 73736 | tf_op jit(solution)/shard_map/ppermute | solution.py:21
  549.4 13.5 %collective-permute-start.93 = (f32[3,32,1,128]{3,2,1,0:T(1,128)}, f32[3,32,1,128]{3,2,1,0:T(1,128)S(1)}, u32[]{:S(2)}, u32[]{:S(2)}) collective-permute-start(f32[3,32,1,128]{3,2,1,0:T(1,128)} %get-tuple-element.51), channel_id=1, source_target_pairs={{0,2},{2,4},{4,6},{1,3},{3,5},{5,7},{8,10},{10,12},{12,14},{9,11},... | collective-permute-start | bytes 147464 | tf_op jit(solution)/shard_map/ppermute | solution.py:21
  553.9 9.0 %collective-permute-start.92 = (f32[3,32,1,128]{3,2,1,0:T(1,128)S(1)}, f32[3,32,1,128]{3,2,1,0:T(1,128)S(1)}, u32[]{:S(2)}, u32[]{:S(2)}) collective-permute-start(f32[3,32,1,128]{3,2,1,0:T(1,128)S(1)} %get-tuple-element.52), channel_id=1, source_target_pairs={{2,0},{4,2},{6,4},{3,1},{5,3},{7,5},{10,8},{12,10},{14,12},{11,9},... | collective-permute-start | bytes 147464 | tf_op jit(solution)/shard_map/ppermute | solution.py:21
  566.9 13.8 %collective-permute-start.96 = (f32[1,16,128]{2,1,0:T(8,128)S(1)}, f32[1,16,128]{2,1,0:T(8,128)S(1)}, u32[]{:S(2)}, u32[]{:S(2)}) collective-permute-start(f32[1,16,128]{2,1,0:T(8,128)S(1)} %slice_bitcast_fusion.16), channel_id=1, source_target_pairs={{0,8},{8,16},{16,24},{1,9},{9,17},{17,25},{2,10},{10,18},{18,26},{... | collective-permute-start | bytes 24584 | tf_op jit(solution)/shard_map/ppermute | solution.py:21
  571.6 9.1 %collective-permute-start.97 = (f32[32,1,128]{2,1,0:T(1,128)S(1)}, f32[32,1,128]{2,1,0:T(1,128)S(1)}, u32[]{:S(2)}, u32[]{:S(2)}) collective-permute-start(f32[32,1,128]{2,1,0:T(1,128)S(1)} %slice.1226), channel_id=1, source_target_pairs={{0,2},{2,4},{4,6},{1,3},{3,5},{5,7},{8,10},{10,12},{12,14},{9,11},... | collective-permute-start | bytes 49160 | tf_op jit(solution)/shard_map/ppermute | solution.py:21
  (107 other events, 658.2 us)
